TPU v7x, 32 devices: a whole 2x2x4 slice. The times are simulated.
32 devices in a mesh: rep: 16 (over z, x, core), fsdp: 2 (over y).
Axes of the slice: x: 2, y: 2, z: 4, core: 2. Of those that a mesh axis runs over, the one named last changes fastest.
Arguments:
- hidden: bfloat16 [4096, 8192], P(('rep', 'fsdp')), may hold values from -6 to 6
- local_weight: bfloat16 [16, 8192, 2048], P('rep', 'fsdp'), may hold values from -0.09375 to 0.09375
- master: float32 [8192, 2048], P('fsdp', 'rep'), may hold values from -0.0625 to 0.0625
- momentum: float32 [8192, 2048], P('fsdp', 'rep'), may hold values from -0.06 to 0.06
- dither: int32 [16, 8192, 16], P('rep', 'fsdp'), may hold values from 0 to 15
Outputs:
- key_values: bfloat16 [4096, 2048], P(('rep', 'fsdp'))
- new_master: float32 [8192, 2048], P('fsdp', 'rep')
- new_momentum: float32 [8192, 2048], P('fsdp', 'rep')
- new_local: bfloat16 [16, 8192, 2048], P('rep', 'fsdp')
All inputs are finite; a program needn't handle non-finite values.
Results may differ from a plain program's by a relative error of at most 0.0067.
Values may be sent and summed in bfloat16 or wider, within the bound.
No kernel may reach another device: no remote copies, remote signals or barrier semaphores. Data moves between devices by JAX's collectives and lax.ppermute only.
A program may use at most 192 MiB of HBM per device.

v0:
```python
import math

import jax
import jax.numpy as jnp
from jax import lax
from jax.sharding import PartitionSpec as P

BLOCK = 128


momentum_keep = 0.9
outer_rate = 0.7
mix_share = 0.5


def code_block(delta, dither):
    row_count = delta.shape[0]
    blocked = delta.reshape(row_count, -1, BLOCK)
    scaling = (jnp.max(jnp.abs(blocked), axis=2, keepdims=True) + 1e-06) / 7.0
    offset = (dither.astype(jnp.float32)[:, :, None] + 0.5) / 16.0 - 0.5
    levels = jnp.clip(blocked / scaling + offset, -8.0, 7.0)
    smooth = levels - jnp.sin(2.0 * math.pi * levels) / (2.0 * math.pi)
    return (scaling * (smooth - offset)).reshape(row_count, -1)


def shards(hidden, local_weight, master, momentum, dither):
    weights = local_weight[0]
    key_values = jnp.dot(
        hidden,
        lax.all_gather(weights, "fsdp", axis=0, tiled=True),
        preferred_element_type=jnp.float32,
    ).astype(jnp.bfloat16)
    anchor = lax.all_gather(master.astype(jnp.bfloat16), "rep", axis=1, tiled=True)
    delta = anchor.astype(jnp.float32) - weights.astype(jnp.float32)
    coded = code_block(delta, dither[0]).astype(jnp.bfloat16)
    replicas = lax.axis_size("rep")
    widened = lax.optimization_barrier(coded).astype(jnp.float32)
    summed = lax.psum_scatter(widened, "rep", scatter_dimension=1, tiled=True)
    averaged = summed / replicas
    new_momentum = momentum_keep * momentum + averaged
    new_master = master - outer_rate * (averaged + momentum_keep * new_momentum)
    gathered = lax.all_gather(new_master.astype(jnp.bfloat16), "rep", axis=1, tiled=True)
    merged = mix_share * weights.astype(jnp.float32) + (1.0 - mix_share) * gathered.astype(
        jnp.float32
    )
    new_local = merged.astype(jnp.bfloat16)[None]
    return (key_values, new_master, new_momentum, new_local)


def solution(mesh):
    return jax.shard_map(
        shards,
        mesh=mesh,
        in_specs=(
            P(("rep", "fsdp"), None),
            P("rep", "fsdp", None),
            P("fsdp", "rep"),
            P("fsdp", "rep"),
            P("rep", "fsdp", None),
        ),
        out_specs=(
            P(("rep", "fsdp"), None),
            P("fsdp", "rep"),
            P("fsdp", "rep"),
            P("rep", "fsdp", None),
        ),
        check_vma=False,
    )
```

profile of v0, /device:TPU:0, one launch (start us, length us, event | category | flops | bytes accessed | tf_op | source)
XLA Modules:
  0.0 924.9 jit_solution(2626235479547939231)
XLA Ops:
  8.0 0.0 copy-start
  8.0 0.0 all-gather.5.cloned.1.call-start
  8.1 2.8 convert_element_type.37
  10.9 0.0 all-gather.5.cloned.1.call-update
  10.9 0.0 reduce-scatter.2.cloned.1.call-start
  10.9 1.0 add_bitcast_fusion
  11.9 1.9 copy.9
  13.9 130.3 %all-gather.5.cloned.1.call-done = bf16[4096,2048]{1,0:T(8,128)(2,1)} async-done(((bf16[4096,128]{1,0:T(8,128)(2,1)}), bf16[4096,2048]{1,0:T(8,128)(2,1)}) %all-gather.5.cloned.1.call-update) | async-done | bytes 16777232 | tf_op jit(solution)/shard_map/all_gather | solution.py:33
  144.2 14.2 %abs_bitcast_fusion = f32[512,8,16,128]{3,1,2,0:T(8,128)S(1)} fusion(bf16[4096,2048]{1,0:T(8,128)(2,1)} %all-gather.5.cloned.1.call-done, bf16[1,4096,2048]{2,1,0:T(8,128)(2,1)} %param.6), kind=kLoop, calls=%fused_computation.12 | loop fusion | flops 33554432 | bytes 67108864
  158.4 13.7 %copy.10 = f32[512,8,16,128]{3,2,1,0:T(8,128)} copy(f32[512,8,16,128]{3,1,2,0:T(8,128)S(1)} %abs_bitcast_fusion) | data formatting | bytes 67108864
  172.1 16.7 %reduce_max.9 = f32[4096,16]{1,0:T(8,128)} reduce(f32[4096,16,128]{2,1,0:T(8,128)} %bitcast.42, f32[]{:T(128)} %constant.5.clone.1), dimensions={2}, to_apply=%region_0.0 | reduce | flops 8323072 | bytes 33816580 | tf_op jit(solution)/shard_map/reduce_max | solution.py:19
  188.8 1.9 add_multiply_fusion
  190.7 0.0 copy-start.1
  190.7 0.0 slice-start
  190.7 0.0 slice-start.1
  190.7 17.0 %mul.31 = f32[4096,16,128]{2,1,0:T(8,128)} broadcast(f32[4096,16]{1,0:T(8,128)S(1)} %add_multiply_fusion), dimensions={0,1} | broadcast | bytes 33816576 | tf_op jit(solution)/shard_map/mul | solution.py:23
  207.7 0.0 copy-done.1
  207.7 17.0 %add.53 = f32[4096,16,128]{2,1,0:T(8,128)} broadcast(f32[4096,16]{1,0:T(8,128)S(1)} %copy-done.1), dimensions={0,1} | broadcast | bytes 33816576 | tf_op jit(solution)/shard_map/add | solution.py:21
  224.6 0.0 slice-done
  224.7 133.2 %fusion.4 = bf16[4096,2048]{1,0:T(8,128)(2,1)} fusion(f32[512,8,16,128]{3,2,1,0:T(8,128)} %bitcast.41, f32[512,8,16,128]{3,2,1,0:T(8,128)} %bitcast.40, bf16[4096,2048]{1,0:T(8,128)(2,1)} %all-gather.5.cloned.1.call-done, bf16[1,4096,2048]{2,1,0:T(8,128)(2,1)S(1)} %bitcast.39), kind=kLoop, calls=%fused_computation.8 | loop fusion | flops 100663296 | bytes 117440512 | tf_op jit(solution)/shard_map/convert_element_type | solution.py:35
  357.9 18.7 %convert_element_type.42 = f32[4096,2048]{1,0:T(8,128)} convert(bf16[4096,2048]{1,0:T(8,128)(2,1)} %fusion.4) | non-fusion elementwise | flops 8388608 | bytes 50331648 | tf_op jit(solution)/shard_map/convert_element_type | solution.py:37
  376.6 0.0 reduce-scatter.2.cloned.1.call-update
  376.6 0.0 all-gather.9.cloned.1.call-start
  376.7 0.5 all-gather.9.cloned.1.call-update
  377.2 0.2 all-gather.7.cloned.1.call-start
  377.5 327.8 %reduce-scatter.2.cloned.1.call-done = f32[4096,128]{1,0:T(8,128)} async-done(((f32[4096,2048]{1,0:T(8,128)}), f32[4096,128]{1,0:T(8,128)}) %reduce-scatter.2.cloned.1.call-update) | async-done | bytes 2097168 | tf_op jit(solution)/shard_map/reduce_scatter | solution.py:38
  705.2 5.8 fusion.11
  711.0 0.0 all-gather.7.cloned.1.call-update
  711.0 54.2 %all-gather.9.cloned.1.call-done = bf16[1,8192,2048]{2,1,0:T(8,128)(2,1)} async-done(((bf16[1,4096,2048]{2,1,0:T(8,128)(2,1)}), bf16[1,8192,2048]{2,1,0:T(8,128)(2,1)}) %all-gather.9.cloned.1.call-update) | async-done | bytes 33554448 | tf_op jit(solution)/shard_map/all_gather | solution.py:30
  765.3 14.1 %fusion.8 = bf16[128,2048]{1,0:T(8,128)(2,1)} fusion(bf16[128,8192]{1,0:T(8,128)(2,1)S(1)} %copy-done, bf16[1,8192,2048]{2,1,0:T(8,128)(2,1)} %all-gather.9.cloned.1.call-done), kind=kOutput, calls=%fused_computation.14 | convolution fusion | flops 4295229440 | bytes 36175872 | tf_op jit(solution)/shard_map/dot_general | solution.py:28
  779.4 118.2 %all-gather.7.cloned.1.call-done = bf16[4096,2048]{1,0:T(8,128)(2,1)} async-done(((bf16[4096,128]{1,0:T(8,128)(2,1)}), bf16[4096,2048]{1,0:T(8,128)(2,1)}) %all-gather.7.cloned.1.call-update) | async-done | bytes 16777232 | tf_op jit(solution)/shard_map/all_gather | solution.py:42
  897.6 19.9 %fusion.7 = bf16[1,4096,2048]{2,1,0:T(8,128)(2,1)} fusion(bf16[4096,2048]{1,0:T(8,128)(2,1)} %all-gather.7.cloned.1.call-done, bf16[1,4096,2048]{2,1,0:T(8,128)(2,1)} %param.6), kind=kLoop, calls=%fused_computation.13 | loop fusion | flops 41943040 | bytes 50331648 | tf_op jit(solution)/shard_map/broadcast_in_dim | solution.py:46
  (7 shorter events, 0.0 us)
Async XLA Ops:
  8.0 757.3 %copy-start = (bf16[128,8192]{1,0:T(8,128)(2,1)S(1)}, bf16[128,8192]{1,0:T(8,128)(2,1)}, u32[]{:S(2)}) copy-start(bf16[128,8192]{1,0:T(8,128)(2,1)} %param.5) | copy-start | bytes 6291460
  8.0 136.2 %all-gather.5.cloned.1.call-start = ((), (), s32[]{:S(2)}) async-start(), calls=%async_computation.1 | async-start | bytes 17825792 | tf_op jit(solution)/shard_map/all_gather | solution.py:33
  10.9 694.3 %reduce-scatter.2.cloned.1.call-start = ((), (), s32[]{:S(2)}) async-start(), calls=%async_computation.2 | async-start | bytes 35651584 | tf_op jit(solution)/shard_map/reduce_scatter | solution.py:38
  190.7 17.0 %copy-start.1 = (f32[4096,16]{1,0:T(8,128)S(1)}, f32[4096,16]{1,0:T(8,128)}, u32[]{:S(2)}) copy-start(f32[4096,16]{1,0:T(8,128)} %copy.9) | copy-start | bytes 786436
  190.7 34.0 %slice-start = ((s8[16777216]{0:T(1024)(128)(4,1)}), s8[4194304]{0:T(1024)(128)(4,1)S(1)}, s32[]{:S(2)}) async-start(s8[16777216]{0:T(1024)(128)(4,1)} %bitcast.38), calls=%async_computation.5 | async-start | bytes 8388608
  190.7 34.0 %slice-start.1 = ((s8[16777216]{0:T(1024)(128)(4,1)}), s8[4194304]{0:T(1024)(128)(4,1)S(1)}, s32[]{:S(2)}) async-start(s8[16777216]{0:T(1024)(128)(4,1)} %bitcast.38), calls=%async_computation.6 | async-start | bytes 8388608
  207.7 17.0 %slice-start.2 = ((s8[16777216]{0:T(1024)(128)(4,1)}), s8[4194304]{0:T(1024)(128)(4,1)S(1)}, s32[]{:S(2)}) async-start(s8[16777216]{0:T(1024)(128)(4,1)} %bitcast.38), calls=%async_computation.7 | async-start | bytes 8388608
  207.7 17.0 %slice-start.3 = ((s8[16777216]{0:T(1024)(128)(4,1)}), s8[4194304]{0:T(1024)(128)(4,1)S(1)}, s32[]{:S(2)}) async-start(s8[16777216]{0:T(1024)(128)(4,1)} %bitcast.38), calls=%async_computation.8 | async-start | bytes 8388608
  376.6 388.6 %all-gather.9.cloned.1.call-start = ((), (), s32[]{:S(2)}) async-start(), calls=%async_computation.4 | async-start | bytes 50331648 | tf_op jit(solution)/shard_map/all_gather | solution.py:30
  377.2 520.4 %all-gather.7.cloned.1.call-start = ((), (), s32[]{:S(2)}) async-start(), calls=%async_computation.3 | async-start | bytes 17825792 | tf_op jit(solution)/shard_map/all_gather | solution.py:42
Sparse Core Ops, SparseCore 0:
  11.5 132.5 all-gather.4
  376.8 328.4 reduce-scatter.1
Sparse Core Ops, SparseCore 1:
  378.7 386.6 all-gather.8
  767.9 129.7 all-gather.6
where the time goes:
time: 925 us
  waiting for transfers between devices  631 us (68%)
  other arithmetic  214 us (23%)
  local copies, waits for them, and re-layouts  49.6 us (5%)
  between operations  15.6 us (2%)
  matrix products  14.1 us (2%)
    reduce_scatter x1, waiting for transfers between devices, shards(): summed = lax.psum_scatter(widened, 'rep', scatter_dimension=1, tiled=True)  328 us
    convert_element_type x1, other arithmetic, shards(): coded = code_block(delta, dither[0]).astype(jnp.bfloat16)  133 us
    all_gather x1, waiting for transfers between devices, shards(): lax.all_gather(master.astype(jnp.bfloat16), 'rep', axis=1, tiled=True)  130 us
    all_gather x1, waiting for transfers between devices, shards(): lax.all_gather(new_master.astype(jnp.bfloat16), 'rep', axis=1, tiled=True)  118 us
    all_gather x1, waiting for transfers between devices, shards(): lax.all_gather(weights, 'fsdp', axis=0, tiled=True)  54.2 us
    broadcast_in_dim x1, other arithmetic, shards(): new_local = merged.astype(jnp.bfloat16)[None]  19.9 us
    convert_element_type x1, other arithmetic, shards(): widened = lax.optimization_barrier(coded).astype(jnp.float32)  18.7 us
  transfers between devices with their start and end apart: 4, of which 4 were waited for; matrix products, arithmetic and copies ran while one was open for 2% of the time, Pallas kernels for 0%

commit v1 on v0

v1 whole, which is shorter than its diff:
```python
import functools
import math

import jax
import jax.numpy as jnp
from jax import lax
from jax.experimental import pallas as pl
from jax.experimental.pallas import tpu as pltpu
from jax.sharding import PartitionSpec as P

BLOCK = 128
momentum_keep = 0.9
outer_rate = 0.7
mix_share = 0.5

RESIDUE = (
    6.579736255284624,
    -12.98787530573671,
    12.207952703195676,
    -6.691029741717024,
    2.3803828656044055,
    -0.5278879155971964,
)

CHUNKS = 4
TILE = 256
STRIP = 16
MERGE_TILE = 256


def f32(array):
    return array.astype(jnp.float32)


def coded_strip(anchor, weights, offset):
    delta = anchor - f32(weights)
    scaling = (jnp.max(jnp.abs(delta), axis=1, keepdims=True) + 1e-06) * (1.0 / 7.0)
    levels = jnp.clip(delta * (1.0 / scaling) + offset, -8.0, 7.0)
    whole = jnp.round(levels)
    rest = levels - whole
    square = rest * rest
    q = jnp.full_like(square, RESIDUE[-1])
    for coefficient in RESIDUE[-2::-1]:
        q = q * square + coefficient
    smooth = whole + rest * square * q
    return f32((scaling * (smooth - offset)).astype(jnp.bfloat16))


def code_kernel(where_ref, anchor_ref, *refs, strip, first):
    slots, tile, width = anchor_ref.shape
    own_refs, mate_refs = refs[:slots], refs[slots : 2 * slots]
    own_off, mate_off, out_ref, own_wide, mate_wide = refs[2 * slots :]
    per = width // BLOCK
    blocks = own_off.shape[1]
    lane_block = lax.broadcasted_iota(jnp.int32, (blocks, width), 1) // BLOCK
    block = lax.broadcasted_iota(jnp.int32, (blocks, width), 0)
    for s in range(slots):
        pick = (block == lane_block + (first + s * per)).astype(jnp.bfloat16)
        own_wide[s] = jnp.dot(own_off[...], pick, preferred_element_type=jnp.float32)
        mate_wide[s] = jnp.dot(mate_off[...], pick, preferred_element_type=jnp.float32)

    def step(i, carry):
        rows = pl.ds(pl.multiple_of(i * strip, strip), strip)
        for s in range(slots):
            for b in range(per):
                lanes = slice(b * BLOCK, (b + 1) * BLOCK)
                anchor = f32(anchor_ref[s, rows, lanes])
                total = coded_strip(anchor, own_refs[s][rows, lanes], own_wide[s, rows, lanes])
                total += coded_strip(anchor, mate_refs[s][rows, lanes], mate_wide[s, rows, lanes])
                out_ref[s, rows, lanes] = total.astype(out_ref.dtype)
        return carry

    lax.fori_loop(0, tile // strip, step, 0)


def code(where, anchor, weights, mate, own_off, mate_off, group, row):
    slots, rows, width = anchor.shape
    half = weights.shape[0] // 2
    tile = min(TILE, rows)
    strip = min(STRIP, tile)
    blocks = own_off.shape[1]
    row_of = lambda i, w: w[0] * (half // tile) + row // tile + i
    column = lambda s: 1 + group * slots + s
    in_specs = [pl.BlockSpec((slots, tile, width), lambda i, w: (0, i, 0))]
    in_specs += [pl.BlockSpec((tile, width), lambda i, w, s=s: (row_of(i, w), w[column(s)])) for s in range(slots)]
    in_specs += [pl.BlockSpec((tile, width), lambda i, w, s=s: (i, w[column(s)])) for s in range(slots)]
    in_specs += [
        pl.BlockSpec((tile, blocks), lambda i, w: (row_of(i, w), 0)),
        pl.BlockSpec((tile, blocks), lambda i, w: (row // tile + i, 0)),
    ]
    return pl.pallas_call(
        functools.partial(code_kernel, strip=strip, first=group * slots * (width // BLOCK)),
        out_shape=jax.ShapeDtypeStruct(anchor.shape, jnp.bfloat16),
        grid_spec=pltpu.PrefetchScalarGridSpec(
            num_scalar_prefetch=1,
            grid=(rows // tile,),
            in_specs=in_specs,
            out_specs=pl.BlockSpec((slots, tile, width), lambda i, w: (0, i, 0)),
            scratch_shapes=[pltpu.VMEM((slots, tile, width), jnp.float32)] * 2,
        ),
        name="code_pair",
        compiler_params=pltpu.CompilerParams(dimension_semantics=("arbitrary",)),
        cost_estimate=pl.CostEstimate(flops=80 * anchor.size, transcendentals=0, bytes_accessed=8 * anchor.size),
    )(where, anchor, *([weights] * slots), *([mate] * slots), own_off, mate_off)


def merge_kernel(where_ref, *refs, groups):
    fresh, weights_ref, out_ref = refs[:groups], refs[groups], refs[-1]
    slots, _, width = fresh[0].shape
    for g in range(groups):
        for s in range(slots):
            lanes = pl.ds(pl.multiple_of(where_ref[1 + g * slots + s] * width, width), width)
            both = f32(weights_ref[:, lanes]) * mix_share + f32(fresh[g][s]) * (1.0 - mix_share)
            out_ref[:, lanes] = both.astype(out_ref.dtype)


def merge(where, fresh, weights, row, mine, so_far):
    slots, rows, width = fresh[0].shape
    half = weights.shape[0] // 2
    tile = min(MERGE_TILE, rows)

    def place(i, w):
        return ((w[0] if mine else 1 - w[0]) * (half // tile) + row // tile + i, 0)

    full = pl.BlockSpec((tile, weights.shape[1]), place)
    operands = [where, *fresh, weights]
    in_specs = [pl.BlockSpec((slots, tile, width), lambda i, w: (0, i, 0))] * len(fresh) + [full]
    aliases = {}
    if so_far is not None:
        aliases = {len(operands): 0}
        operands.append(so_far)
        in_specs.append(pl.BlockSpec(memory_space=pl.ANY))
    return pl.pallas_call(
        functools.partial(merge_kernel, groups=len(fresh)),
        out_shape=jax.ShapeDtypeStruct(weights.shape, jnp.bfloat16),
        grid_spec=pltpu.PrefetchScalarGridSpec(
            num_scalar_prefetch=1, grid=(rows // tile,), in_specs=in_specs, out_specs=full
        ),
        input_output_aliases=aliases,
        name="merge_rows",
        compiler_params=pltpu.CompilerParams(dimension_semantics=("arbitrary",)),
        cost_estimate=pl.CostEstimate(
            flops=4 * rows * weights.shape[1], transcendentals=0, bytes_accessed=6 * rows * weights.shape[1]
        ),
    )(*operands)


class Line:
    def __init__(self, total, length, stride):
        self.length = length
        self.stride = stride
        self.position = (lax.axis_index("rep") // stride) % length
        self.total = total

    def send(self, array, by):
        def target(i):
            n = (i // self.stride) % self.length
            return i + ((n + by) % self.length - n) * self.stride

        return lax.ppermute(array, "rep", [(i, target(i)) for i in range(self.total)])

    def gather(self, array):
        return [array] + [self.send(array, -d) for d in range(1, self.length)]

    def reduce(self, slots):
        arrived = [self.send(slots[d], d) for d in range(1, self.length)]
        return sum((f32(a) for a in arrived), f32(slots[0]))


def project(hidden, weights):
    share = lax.axis_size("fsdp")
    place = lax.axis_index("fsdp")
    depth = weights.shape[0]
    tokens = hidden.shape[0]

    def columns(at):
        return lax.dynamic_slice(hidden, (0, at % share * depth), (tokens, depth))

    def shifted(array, by):
        return lax.ppermute(array, "fsdp", [(i, (i + by) % share) for i in range(share)])

    gathered = [columns(place)] + [shifted(columns(place + s), s) for s in range(1, share)]
    partial = jnp.dot(jnp.concatenate(gathered), weights, preferred_element_type=jnp.float32)
    total = partial[:tokens]
    for s in range(1, share):
        total += shifted(partial[s * tokens : (s + 1) * tokens], -s)
    return total.astype(jnp.bfloat16)


def shards(hidden, local_weight, master, momentum, dither):
    weights = local_weight[0]
    rows, columns = weights.shape
    replicas = lax.axis_size("rep")
    chips = replicas // 2
    x_length = 2 ** int(math.log2(chips) / 2)
    z_length = chips // x_length
    core = lax.axis_index("rep") % 2
    x_line = Line(replicas, x_length, 2)
    z_line = Line(replicas, z_length, 2 * x_length)
    half = rows // 2
    piece = half // CHUNKS
    width = columns // chips
    mine, theirs = core * half, (1 - core) * half

    def swap(array):
        return lax.ppermute(array, "rep", [(i, i ^ 1) for i in range(replicas)])

    def halves(array, start, count=half):
        return lax.dynamic_slice(array, (start, 0), (count, array.shape[1]))

    def beside(own, other):
        return jnp.where(core == 0, jnp.concatenate([own, other], 1), jnp.concatenate([other, own], 1))

    rounded = master.astype(jnp.bfloat16)
    anchor = beside(halves(rounded, mine), swap(halves(rounded, theirs)))
    parts = [slice(i * piece, (i + 1) * piece) for i in range(CHUNKS)]

    groups = []
    for part in parts:
        pieces = z_line.gather(anchor[part])
        groups.append(x_line.gather(jnp.stack(pieces)))

    d = jnp.arange(z_length, dtype=jnp.int32)[None, :]
    e = jnp.arange(x_length, dtype=jnp.int32)[:, None]
    places = (((z_line.position + d) % z_length) * x_length + (x_line.position + e) % x_length).reshape(-1)
    where = jnp.concatenate([core[None].astype(jnp.int32), places])

    offset = (f32(dither[0]) + 0.5) / 16.0 - 0.5
    block_places = (places[:, None] * (width // BLOCK) + jnp.arange(width // BLOCK)[None, :]).reshape(-1)
    pick = jnp.arange(offset.shape[1])[:, None] == block_places[None, :]
    offset = jnp.dot(offset.astype(jnp.bfloat16), pick.astype(jnp.bfloat16), preferred_element_type=jnp.float32)
    offset = offset.astype(jnp.bfloat16)
    mate_offset = swap(halves(offset, theirs))
    mates = [swap(halves(weights, theirs + i * piece, piece)) for i in range(CHUNKS)]
    pair_master = beside(halves(master, mine), swap(halves(master, theirs)))
    pair_momentum = beside(halves(momentum, mine), swap(halves(momentum, theirs)))
    key_values = project(hidden, weights)

    masters, momenta, fresh, swapped = [], [], [], []
    for i, part in enumerate(parts):
        sums = [None] * x_length
        for g in reversed(range(x_length)):
            sums[g] = code(where, groups[i][g], weights, mates[i], offset, mate_offset, g, i * piece)
        summed = x_line.reduce(sums).astype(jnp.bfloat16)
        averaged = z_line.reduce([summed[k] for k in range(z_length)]) / replicas
        old_master, old_momentum, *_ = lax.optimization_barrier((pair_master[part], pair_momentum[part], *masters[-1:]))
        new_momentum = momentum_keep * old_momentum + averaged
        new_master = old_master - outer_rate * (averaged + momentum_keep * new_momentum)
        masters.append(new_master)
        momenta.append(new_momentum)
        pieces = z_line.gather(new_master.astype(jnp.bfloat16))
        fresh.append(x_line.gather(jnp.stack(pieces)))
        swapped.append([swap(group) for group in fresh[-1]])

    def home(pieces):
        pair = jnp.concatenate(pieces)
        own = pair.shape[1] // 2
        left, right = pair[:, :own], pair[:, own:]
        keep, give = jnp.where(core == 0, left, right), jnp.where(core == 0, right, left)
        got = swap(give)
        return jnp.where(core == 0, jnp.concatenate([keep, got]), jnp.concatenate([got, keep]))

    final_master, final_momentum = home(masters), home(momenta)
    new_local = None
    for i in range(CHUNKS + 1):
        if i < CHUNKS:
            new_local = merge(where, fresh[i], weights, i * piece, True, new_local)
        if i > 0:
            new_local = merge(where, swapped[i - 1], weights, (i - 1) * piece, False, new_local)
    return (key_values, final_master, final_momentum, new_local[None])


def solution(mesh):
    return jax.shard_map(
        shards,
        mesh=mesh,
        in_specs=(
            P(("rep", "fsdp"), None),
            P("rep", "fsdp", None),
            P("fsdp", "rep"),
            P("fsdp", "rep"),
            P("rep", "fsdp", None),
        ),
        out_specs=(
            P(("rep", "fsdp"), None),
            P("fsdp", "rep"),
            P("fsdp", "rep"),
            P("rep", "fsdp", None),
        ),
        check_vma=False,
    )
```

time: 925 us -> 558 us (0.60)
  waiting for transfers between devices: 631 us -> 203 us
  other arithmetic: 214 us -> 23.5 us
  starting transfers between devices: 0.35 us -> 172 us
  Pallas kernels: 0 us -> 119 us
  local copies, waits for them, and re-layouts: 49.6 us -> 23.9 us
  between operations: 15.6 us -> 1.2 us
    reduce_scatter x1 -> x0, waiting for transfers between devices: 328 us -> none  [shards(): summed = lax.psum_scatter(widened, 'rep', scatter_dimension=1, tiled=True)]
    all_gather x3 -> x0, waiting for transfers between devices: 303 us -> none  [the longest x1 130 us: shards(): lax.all_gather(master.astype(jnp.bfloat16), 'rep', axis=1, tiled=True)]
    ppermute x0 -> x68, waiting for transfers between devices: none -> 203 us  [the longest x48 185 us: send(): lax.ppermute(array, 'rep', [(i, target(i)) for i in range(self.total)])]
    ppermute x0 -> x68, starting transfers between devices: none -> 172 us  [the longest x48 165 us: send(): lax.ppermute(array, 'rep', [(i, target(i)) for i in range(self.total)])]
    convert_element_type x4 -> x10, other arithmetic: 161 us -> 8.64 us  [the longest x4 4.85 us: shards(): summed = x_line.reduce(sums).astype(jnp.bfloat16)]
    pallas_call x0 -> x16, Pallas kernels: none -> 119 us  [the longest x8 85.3 us: code(): pl.pallas_call(functools.partial(code_kernel, strip=strip, first=group *...]
    broadcast_in_dim x1 -> x0, other arithmetic: 19.9 us -> none  [shards(): new_local = merged.astype(jnp.bfloat16)[None]]
    mul x1 -> x0, local copies, waits for them, and re-layouts: 17 us -> none  [code_block(): return (scaling * (smooth - offset)).reshape(row_count, -1)]
  transfers between devices with their start and end apart: 4 -> 68, of which waited for: 4 -> 25; matrix products, arithmetic and copies ran while one was open for 2% -> 10% of each run, Pallas kernels for 0% -> 21%
where the time goes in v1:
time: 558 us; the launch traced here: 557 us
  waiting for transfers between devices  203 us (36%)
  starting transfers between devices  172 us (31%)
  Pallas kernels  119 us (21%)
  local copies, waits for them, and re-layouts  23.9 us (4%)
  other arithmetic  23.5 us (4%)
  matrix products  13.8 us (2%)
    ppermute x48, waiting for transfers between devices, send(): lax.ppermute(array, 'rep', [(i, target(i)) for i in range(self.total)])  185 us
    ppermute x48, starting transfers between devices, send(): lax.ppermute(array, 'rep', [(i, target(i)) for i in range(self.total)])  165 us
    pallas_call x8, Pallas kernels, code(): pl.pallas_call(functools.partial(code_kernel, strip=strip, first=group *...  85.3 us
    pallas_call x8, Pallas kernels, merge(): pl.pallas_call(functools.partial(merge_kernel, groups=len(fresh)), out_sh...  33.9 us
    ppermute x2, waiting for transfers between devices, shifted(): lax.ppermute(array, 'fsdp', [(i, (i + by) % share) for i in range(share)])  17.2 us
    dot_general x1, matrix products, project(): jnp.dot(jnp.concatenate(gathered), weights, preferred_element_type=jnp.fl...  12.4 us
    dynamic_slice x5, local copies, waits for them, and re-layouts, halves(): return lax.dynamic_slice(array, (start, 0), (count, array.shape[1]))  11.3 us
  transfers between devices with their start and end apart: 68, of which 25 were waited for; matrix products, arithmetic and copies ran while one was open for 10% of the time, Pallas kernels for 21%

profile of v1, /device:TPU:0, one launch (start us, length us, event | category | flops | bytes accessed | tf_op | source)
XLA Modules:
  0.0 556.9 jit_solution(16391570376504127976)
XLA Ops:
  3.7 7.5 %dynamic-slice_bitcast_fusion = (bf16[512,2048]{1,0:T(8,128)(2,1)}, bf16[512,2048]{1,0:T(8,128)(2,1)}, bf16[512,2048]{1,0:T(8,128)(2,1)}, bf16[512,2048]{1,0:T(8,128)(2,1)}) fusion(bf16[1,4096,2048]{2,1,0:T(8,128)(2,1)} %param.6, s32[]{:T(128)S(6)} %select_n.150, s32[]{:T(128)S(6)} %select_n.148, s32[]{:T(128)S(6)} %select_n.138, s32[]{:T(128)S(6)} %select_n.149), kind=kLoop, calls=%fused_computation.12 | loop fusion | bytes 16777232 | tf_op jit(solution)/shard_map/dynamic_slice | solution.py:209
  26.7 16.1 %collective-permute-done.6 = bf16[512,256]{1,0:T(8,128)(2,1)} collective-permute-done((bf16[512,256]{1,0:T(8,128)(2,1)}, bf16[512,256]{1,0:T(8,128)(2,1)}, u32[]{:S(2)}, u32[]{:S(2)}) %collective-permute-start.6) | collective-permute-done | bytes 262176 | tf_op jit(solution)/shard_map/ppermute | solution.py:160
  49.0 15.4 %collective-permute-done.16 = bf16[512,256]{1,0:T(8,128)(2,1)S(1)} collective-permute-done((bf16[512,256]{1,0:T(8,128)(2,1)}, bf16[512,256]{1,0:T(8,128)(2,1)S(1)}, u32[]{:S(2)}, u32[]{:S(2)}) %collective-permute-start.16) | collective-permute-done | bytes 262176 | tf_op jit(solution)/shard_map/ppermute | solution.py:160
  68.8 10.6 %collective-permute-start.26 = (bf16[512,256]{1,0:T(8,128)(2,1)S(1)}, bf16[512,256]{1,0:T(8,128)(2,1)S(1)}, u32[]{:S(2)}, u32[]{:S(2)}) collective-permute-start(bf16[512,256]{1,0:T(8,128)(2,1)S(1)} %copy-done.37), channel_id=1, source_target_pairs={{0,8},{2,10},{4,12},{6,14},{8,16},{10,18},{12,20},{14,22},{16,24},... | collective-permute-start | bytes 786440 | tf_op jit(solution)/shard_map/ppermute | solution.py:160
  79.4 6.9 %collective-permute-done.25 = bf16[512,256]{1,0:T(8,128)(2,1)S(1)} collective-permute-done((bf16[512,256]{1,0:T(8,128)(2,1)S(1)}, bf16[512,256]{1,0:T(8,128)(2,1)S(1)}, u32[]{:S(2)}, u32[]{:S(2)}) %collective-permute-start.25) | collective-permute-done | bytes 262176 | tf_op jit(solution)/shard_map/ppermute | solution.py:160
  94.4 10.3 %collective-permute-start.35 = (bf16[512,256]{1,0:T(8,128)(2,1)S(1)}, bf16[512,256]{1,0:T(8,128)(2,1)S(1)}, u32[]{:S(2)}, u32[]{:S(2)}) collective-permute-start(bf16[512,256]{1,0:T(8,128)(2,1)S(1)} %copy-done.36), channel_id=1, source_target_pairs={{0,8},{2,10},{4,12},{6,14},{8,16},{10,18},{12,20},{14,22},{16,24},... | collective-permute-start | bytes 786440 | tf_op jit(solution)/shard_map/ppermute | solution.py:160
  114.7 10.6 %code_pair.9 = bf16[4,512,256]{2,1,0:T(8,128)(2,1)} custom-call(s32[9]{0:T(128)} %pad_add_fusion.where_ref, bf16[4,512,256]{2,1,0:T(8,128)(2,1)} %copy-done.26, bf16[4096,2048]{1,0:T(8,128)(2,1)} %bitcast.120, bf16[4096,2048]{1,0:T(8,128)(2,1)} %bitcast.121, bf16[4096,2048]{1,0:T(8,128)(2,1)} %bitcast.122, bf16[4096,2048]{1,0:T(8,128)(2,1)} %bitcast.123, ...), custom_call_target="tpu_custom_call" | custom-call | flops 41943040 | bytes 4194304 | tf_op jit(solution)/shard_map/code_pair/pallas_call | solution.py:91
  125.9 8.6 %collective-permute-done = bf16[128,4096]{1,0:T(8,128)(2,1)} collective-permute-done((bf16[128,4096]{1,0:T(8,128)(2,1)}, bf16[128,4096]{1,0:T(8,128)(2,1)}, u32[]{:S(2)}, u32[]{:S(2)}) %collective-permute-start) | collective-permute-done | bytes 1048608 | tf_op jit(solution)/shard_map/ppermute | solution.py:180
  138.1 12.4 %fusion = f32[256,2048]{1,0:T(8,128)} fusion(bf16[128,4096]{1,0:T(8,128)(2,1)} %collective-permute-done, bf16[128,4096]{1,0:T(8,128)(2,1)} %get-tuple-element.52, bf16[1,4096,2048]{2,1,0:T(8,128)(2,1)} %param.6), kind=kOutput, calls=%fused_computation.1 | convolution fusion | flops 4299161600 | bytes 20971520 | tf_op jit(solution)/shard_map/dot_general | solution.py:183
  155.2 10.7 %code_pair.11 = bf16[4,512,256]{2,1,0:T(8,128)(2,1)} custom-call(s32[9]{0:T(128)} %pad_add_fusion.where_ref, bf16[4,512,256]{2,1,0:T(8,128)(2,1)} %collective-permute-done.19.anchor_ref, bf16[4096,2048]{1,0:T(8,128)(2,1)} %bitcast.124, bf16[4096,2048]{1,0:T(8,128)(2,1)} %bitcast.125, bf16[4096,2048]{1,0:T(8,128)(2,1)} %bitcast.126, ...), custom_call_target="tpu_custom_call" | custom-call | flops 41943040 | bytes 4194304 | tf_op jit(solution)/shard_map/code_pair/pallas_call | solution.py:91
  174.4 10.6 %code_pair.13 = bf16[4,512,256]{2,1,0:T(8,128)(2,1)} custom-call(s32[9]{0:T(128)} %pad_add_fusion.where_ref, bf16[4,512,256]{2,1,0:T(8,128)(2,1)} %collective-permute-done.28.anchor_ref, bf16[4096,2048]{1,0:T(8,128)(2,1)} %bitcast.128, bf16[4096,2048]{1,0:T(8,128)(2,1)} %bitcast.129, bf16[4096,2048]{1,0:T(8,128)(2,1)} %bitcast.130, ...), custom_call_target="tpu_custom_call" | custom-call | flops 41943040 | bytes 4194304 | tf_op jit(solution)/shard_map/code_pair/pallas_call | solution.py:91
  186.0 10.7 %code_pair.15 = bf16[4,512,256]{2,1,0:T(8,128)(2,1)} custom-call(s32[9]{0:T(128)} %pad_add_fusion.where_ref, bf16[4,512,256]{2,1,0:T(8,128)(2,1)} %collective-permute-done.37.anchor_ref, bf16[4096,2048]{1,0:T(8,128)(2,1)} %bitcast.132, bf16[4096,2048]{1,0:T(8,128)(2,1)} %bitcast.133, bf16[4096,2048]{1,0:T(8,128)(2,1)} %bitcast.134, ...), custom_call_target="tpu_custom_call" | custom-call | flops 41943040 | bytes 4194304 | tf_op jit(solution)/shard_map/code_pair/pallas_call | solution.py:91
  197.7 10.7 %code_pair.8 = bf16[4,512,256]{2,1,0:T(8,128)(2,1)} custom-call(s32[9]{0:T(128)} %pad_add_fusion.where_ref, bf16[4,512,256]{2,1,0:T(8,128)(2,1)} %copy-done.9, bf16[4096,2048]{1,0:T(8,128)(2,1)} %bitcast.138, bf16[4096,2048]{1,0:T(8,128)(2,1)} %bitcast.137, bf16[4096,2048]{1,0:T(8,128)(2,1)} %bitcast.136, bf16[4096,2048]{1,0:T(8,128)(2,1)} %bitcast.139, ...), custom_call_target="tpu_custom_call" | custom-call | flops 41943040 | bytes 4194304 | tf_op jit(solution)/shard_map/code_pair/pallas_call | solution.py:91
  208.4 10.7 %code_pair.10 = bf16[4,512,256]{2,1,0:T(8,128)(2,1)} custom-call(s32[9]{0:T(128)} %pad_add_fusion.where_ref, bf16[4,512,256]{2,1,0:T(8,128)(2,1)} %copy-done.10, bf16[4096,2048]{1,0:T(8,128)(2,1)} %bitcast.140, bf16[4096,2048]{1,0:T(8,128)(2,1)} %bitcast.141, bf16[4096,2048]{1,0:T(8,128)(2,1)} %bitcast.142, bf16[4096,2048]{1,0:T(8,128)(2,1)} %bitcast.143, ...), custom_call_target="tpu_custom_call" | custom-call | flops 41943040 | bytes 4194304 | tf_op jit(solution)/shard_map/code_pair/pallas_call | solution.py:91
  219.1 10.6 %code_pair.12 = bf16[4,512,256]{2,1,0:T(8,128)(2,1)} custom-call(s32[9]{0:T(128)} %pad_add_fusion.where_ref, bf16[4,512,256]{2,1,0:T(8,128)(2,1)} %pad_maximum_fusion.4.anchor_ref, bf16[4096,2048]{1,0:T(8,128)(2,1)} %bitcast.144, bf16[4096,2048]{1,0:T(8,128)(2,1)} %bitcast.145, bf16[4096,2048]{1,0:T(8,128)(2,1)} %bitcast.146, bf16[4096,2048]{1,0:T(8,128)(2,1)} %bitcast.147, ...), custom_call_target="tpu_custom_call" | custom-call | flops 41943040 | bytes 4194304 | tf_op jit(solution)/shard_map/code_pair/pallas_call | solution.py:91
  229.7 10.8 %code_pair.14 = bf16[4,512,256]{2,1,0:T(8,128)(2,1)} custom-call(s32[9]{0:T(128)} %pad_add_fusion.where_ref, bf16[4,512,256]{2,1,0:T(8,128)(2,1)} %pad_maximum_fusion.5.anchor_ref, bf16[4096,2048]{1,0:T(8,128)(2,1)} %bitcast.148, bf16[4096,2048]{1,0:T(8,128)(2,1)} %bitcast.149, bf16[4096,2048]{1,0:T(8,128)(2,1)} %bitcast.150, bf16[4096,2048]{1,0:T(8,128)(2,1)} %bitcast.151, ...), custom_call_target="tpu_custom_call" | custom-call | flops 41943040 | bytes 4194304 | tf_op jit(solution)/shard_map/code_pair/pallas_call | solution.py:91
  253.4 18.3 %collective-permute-done.38 = bf16[4,512,256]{2,1,0:T(8,128)(2,1)} collective-permute-done((bf16[4,512,256]{2,1,0:T(8,128)(2,1)}, bf16[4,512,256]{2,1,0:T(8,128)(2,1)}, u32[]{:S(2)}, u32[]{:S(2)}) %collective-permute-start.38) | collective-permute-done | bytes 1048608 | tf_op jit(solution)/shard_map/ppermute | solution.py:160
  282.7 6.8 %collective-permute-done.22 = bf16[512,256]{1,0:T(8,128)(2,1)S(1)} collective-permute-done((bf16[512,256]{1,0:T(8,128)(2,1)S(1)}, bf16[512,256]{1,0:T(8,128)(2,1)S(1)}, u32[]{:S(2)}, u32[]{:S(2)}) %collective-permute-start.22) | collective-permute-done | bytes 262176 | tf_op jit(solution)/shard_map/ppermute | solution.py:160
  293.6 11.8 %collective-permute-start.40 = (bf16[512,256]{1,0:T(8,128)(2,1)S(1)}, bf16[512,256]{1,0:T(8,128)(2,1)S(1)}, u32[]{:S(2)}, u32[]{:S(2)}) collective-permute-start(bf16[512,256]{1,0:T(8,128)(2,1)S(1)} %get-tuple-element.56), channel_id=1, source_target_pairs={{0,16},{2,18},{4,20},{6,22},{8,24},{10,26},{12,28},{14,30},{16,0},... | collective-permute-start | bytes 786440 | tf_op jit(solution)/shard_map/ppermute | solution.py:160
  309.7 11.4 %collective-permute-done.31 = bf16[512,256]{1,0:T(8,128)(2,1)S(1)} collective-permute-done((bf16[512,256]{1,0:T(8,128)(2,1)S(1)}, bf16[512,256]{1,0:T(8,128)(2,1)S(1)}, u32[]{:S(2)}, u32[]{:S(2)}) %collective-permute-start.31) | collective-permute-done | bytes 262176 | tf_op jit(solution)/shard_map/ppermute | solution.py:160
  321.0 7.3 %collective-permute-start.62 = (bf16[512,256]{1,0:T(8,128)(2,1)S(1)}, bf16[512,256]{1,0:T(8,128)(2,1)S(1)}, u32[]{:S(2)}, u32[]{:S(2)}) collective-permute-start(bf16[512,256]{1,0:T(8,128)(2,1)S(1)} %get-tuple-element.20), channel_id=1, source_target_pairs={{0,24},{2,26},{4,28},{6,30},{8,0},{10,2},{12,4},{14,6},{16,8},{18,... | collective-permute-start | bytes 786440 | tf_op jit(solution)/shard_map/ppermute | solution.py:160
  328.6 13.7 %collective-permute-start.64 = (bf16[512,256]{1,0:T(8,128)(2,1)S(1)}, bf16[512,256]{1,0:T(8,128)(2,1)S(1)}, u32[]{:S(2)}, u32[]{:S(2)}) collective-permute-start(bf16[512,256]{1,0:T(8,128)(2,1)S(1)} %get-tuple-element.20), channel_id=1, source_target_pairs={{0,8},{2,10},{4,12},{6,14},{8,16},{10,18},{12,20},{14,22},{16,24},... | collective-permute-start | bytes 786440 | tf_op jit(solution)/shard_map/ppermute | solution.py:160
  343.5 7.4 %collective-permute-start.56 = (bf16[512,256]{1,0:T(8,128)(2,1)S(1)}, bf16[512,256]{1,0:T(8,128)(2,1)S(1)}, u32[]{:S(2)}, u32[]{:S(2)}) collective-permute-start(bf16[512,256]{1,0:T(8,128)(2,1)S(1)} %get-tuple-element.23), channel_id=1, source_target_pairs={{0,24},{2,26},{4,28},{6,30},{8,0},{10,2},{12,4},{14,6},{16,8},{18,... | collective-permute-start | bytes 786440 | tf_op jit(solution)/shard_map/ppermute | solution.py:160
  351.6 14.9 %collective-permute-start.58 = (bf16[512,256]{1,0:T(8,128)(2,1)S(1)}, bf16[512,256]{1,0:T(8,128)(2,1)S(1)}, u32[]{:S(2)}, u32[]{:S(2)}) collective-permute-start(bf16[512,256]{1,0:T(8,128)(2,1)S(1)} %get-tuple-element.23), channel_id=1, source_target_pairs={{0,8},{2,10},{4,12},{6,14},{8,16},{10,18},{12,20},{14,22},{16,24},... | collective-permute-start | bytes 786440 | tf_op jit(solution)/shard_map/ppermute | solution.py:160
  373.4 15.7 %collective-permute-start.52 = (bf16[512,256]{1,0:T(8,128)(2,1)S(1)}, bf16[512,256]{1,0:T(8,128)(2,1)S(1)}, u32[]{:S(2)}, u32[]{:S(2)}) collective-permute-start(bf16[512,256]{1,0:T(8,128)(2,1)S(1)} %get-tuple-element.26), channel_id=1, source_target_pairs={{0,8},{2,10},{4,12},{6,14},{8,16},{10,18},{12,20},{14,22},{16,24},... | collective-permute-start | bytes 786440 | tf_op jit(solution)/shard_map/ppermute | solution.py:160
  395.9 15.7 %collective-permute-start.46 = (bf16[512,256]{1,0:T(8,128)(2,1)S(1)}, bf16[512,256]{1,0:T(8,128)(2,1)S(1)}, u32[]{:S(2)}, u32[]{:S(2)}) collective-permute-start(bf16[512,256]{1,0:T(8,128)(2,1)S(1)} %get-tuple-element.29), channel_id=1, source_target_pairs={{0,8},{2,10},{4,12},{6,14},{8,16},{10,18},{12,20},{14,22},{16,24},... | collective-permute-start | bytes 786440 | tf_op jit(solution)/shard_map/ppermute | solution.py:160
  418.6 7.2 %collective-permute-done.45 = bf16[512,256]{1,0:T(8,128)(2,1)S(1)} collective-permute-done((bf16[512,256]{1,0:T(8,128)(2,1)S(1)}, bf16[512,256]{1,0:T(8,128)(2,1)S(1)}, u32[]{:S(2)}, u32[]{:S(2)}) %collective-permute-start.45) | collective-permute-done | bytes 262176 | tf_op jit(solution)/shard_map/ppermute | solution.py:160
  429.1 8.7 %collective-permute-done.1 = f32[128,2048]{1,0:T(8,128)S(1)} collective-permute-done((f32[128,2048]{1,0:T(8,128)S(1)}, f32[128,2048]{1,0:T(8,128)S(1)}, u32[]{:S(2)}, u32[]{:S(2)}) %collective-permute-start.1) | collective-permute-done | bytes 1048608 | tf_op jit(solution)/shard_map/ppermute | solution.py:180
  439.5 12.4 %collective-permute-done.66.refs_1_ = bf16[4,512,256]{2,1,0:T(8,128)(2,1)S(1)} collective-permute-done((bf16[4,512,256]{2,1,0:T(8,128)(2,1)S(1)}, bf16[4,512,256]{2,1,0:T(8,128)(2,1)S(1)}, u32[]{:S(2)}, u32[]{:S(2)}) %collective-permute-start.66) | collective-permute-done | bytes 1048608 | tf_op jit(solution)/shard_map/ppermute | solution.py:160
  453.3 21.1 %collective-permute-done.60.refs_1_ = bf16[4,512,256]{2,1,0:T(8,128)(2,1)} collective-permute-done((bf16[4,512,256]{2,1,0:T(8,128)(2,1)S(1)}, bf16[4,512,256]{2,1,0:T(8,128)(2,1)}, u32[]{:S(2)}, u32[]{:S(2)}) %collective-permute-start.60) | collective-permute-done | bytes 1048608 | tf_op jit(solution)/shard_map/ppermute | solution.py:160
  474.9 22.0 %collective-permute-done.54.refs_1_ = bf16[4,512,256]{2,1,0:T(8,128)(2,1)} collective-permute-done((bf16[4,512,256]{2,1,0:T(8,128)(2,1)}, bf16[4,512,256]{2,1,0:T(8,128)(2,1)}, u32[]{:S(2)}, u32[]{:S(2)}) %collective-permute-start.54) | collective-permute-done | bytes 1048608 | tf_op jit(solution)/shard_map/ppermute | solution.py:160
  497.4 19.1 %collective-permute-done.48.refs_1_ = bf16[4,512,256]{2,1,0:T(8,128)(2,1)} collective-permute-done((bf16[4,512,256]{2,1,0:T(8,128)(2,1)S(1)}, bf16[4,512,256]{2,1,0:T(8,128)(2,1)}, u32[]{:S(2)}, u32[]{:S(2)}) %collective-permute-start.48) | collective-permute-done | bytes 1048608 | tf_op jit(solution)/shard_map/ppermute | solution.py:160
  (246 shorter events, 169.3 us)
Async XLA Ops:
  11.2 99.2 %collective-permute-start.8 = (bf16[512,2048]{1,0:T(8,128)(2,1)}, bf16[512,2048]{1,0:T(8,128)(2,1)S(1)}, u32[]{:S(2)}, u32[]{:S(2)}) collective-permute-start(bf16[512,2048]{1,0:T(8,128)(2,1)} %get-tuple-element.34), channel_id=1, source_target_pairs={{0,2},{2,0},{4,6},{6,4},{8,10},{10,8},{12,14},{14,12},{16,18},{18,... | collective-permute-start | bytes 6291464 | tf_op jit(solution)/shard_map/ppermute | solution.py:206
  25.3 39.1 %collective-permute-start.16 = (bf16[512,256]{1,0:T(8,128)(2,1)}, bf16[512,256]{1,0:T(8,128)(2,1)S(1)}, u32[]{:S(2)}, u32[]{:S(2)}) collective-permute-start(bf16[512,256]{1,0:T(8,128)(2,1)} %get-tuple-element.63), channel_id=1, source_target_pairs={{0,16},{2,18},{4,20},{6,22},{8,24},{10,26},{12,28},{14,30},{16,0},... | collective-permute-start | bytes 786440 | tf_op jit(solution)/shard_map/ppermute | solution.py:160
  44.9 92.1 %collective-permute-start.18 = (bf16[512,2048]{1,0:T(8,128)(2,1)}, bf16[512,2048]{1,0:T(8,128)(2,1)}, u32[]{:S(2)}, u32[]{:S(2)}) collective-permute-start(bf16[512,2048]{1,0:T(8,128)(2,1)} %get-tuple-element.33), channel_id=1, source_target_pairs={{0,2},{2,0},{4,6},{6,4},{8,10},{10,8},{12,14},{14,12},{16,18},{18,... | collective-permute-start | bytes 6291464 | tf_op jit(solution)/shard_map/ppermute | solution.py:206
  64.4 44.5 %collective-permute-start.10 = (bf16[4,512,256]{2,1,0:T(8,128)(2,1)S(1)}, bf16[4,512,256]{2,1,0:T(8,128)(2,1)S(1)}, u32[]{:S(2)}, u32[]{:S(2)}) collective-permute-start(bf16[4,512,256]{2,1,0:T(8,128)(2,1)S(1)} %pad_maximum_fusion.2.anchor_ref), channel_id=1, source_target_pairs={{0,4},{2,6},{4,0},{6,2},{8,12},{10,14},{12,8},{14,10},{16,20},{18,... | collective-permute-start | bytes 3145736 | tf_op jit(solution)/shard_map/ppermute | solution.py:160
  125.4 47.7 %collective-permute-start.27 = (bf16[512,2048]{1,0:T(8,128)(2,1)}, bf16[512,2048]{1,0:T(8,128)(2,1)S(1)}, u32[]{:S(2)}, u32[]{:S(2)}) collective-permute-start(bf16[512,2048]{1,0:T(8,128)(2,1)} %get-tuple-element.35), channel_id=1, source_target_pairs={{0,2},{2,0},{4,6},{6,4},{8,10},{10,8},{12,14},{14,12},{16,18},{18,... | collective-permute-start | bytes 6291464 | tf_op jit(solution)/shard_map/ppermute | solution.py:206
  125.4 60.6 %collective-permute-start.36 = (bf16[512,2048]{1,0:T(8,128)(2,1)}, bf16[512,2048]{1,0:T(8,128)(2,1)}, u32[]{:S(2)}, u32[]{:S(2)}) collective-permute-start(bf16[512,2048]{1,0:T(8,128)(2,1)} %get-tuple-element.32), channel_id=1, source_target_pairs={{0,2},{2,0},{4,6},{6,4},{8,10},{10,8},{12,14},{14,12},{16,18},{18,... | collective-permute-start | bytes 6291464 | tf_op jit(solution)/shard_map/ppermute | solution.py:206
  136.0 50.0 %collective-permute-start.37 = (bf16[4,512,256]{2,1,0:T(8,128)(2,1)}, bf16[4,512,256]{2,1,0:T(8,128)(2,1)}, u32[]{:S(2)}, u32[]{:S(2)}) collective-permute-start(bf16[4,512,256]{2,1,0:T(8,128)(2,1)} %pad_maximum_fusion.5.anchor_ref), channel_id=1, source_target_pairs={{0,4},{2,6},{4,0},{6,2},{8,12},{10,14},{12,8},{14,10},{16,20},{18,... | collective-permute-start | bytes 3145736 | tf_op jit(solution)/shard_map/ppermute | solution.py:160
  137.1 103.4 %collective-permute-start.11 = (bf16[4,512,256]{2,1,0:T(8,128)(2,1)}, bf16[4,512,256]{2,1,0:T(8,128)(2,1)}, u32[]{:S(2)}, u32[]{:S(2)}) collective-permute-start(bf16[4,512,256]{2,1,0:T(8,128)(2,1)} %code_pair.9), channel_id=1, source_target_pairs={{0,4},{2,6},{4,0},{6,2},{8,12},{10,14},{12,8},{14,10},{16,20},{18,... | collective-permute-start | bytes 3145736 | tf_op jit(solution)/shard_map/ppermute | solution.py:160
  165.9 79.0 %collective-permute-start.20 = (bf16[4,512,256]{2,1,0:T(8,128)(2,1)}, bf16[4,512,256]{2,1,0:T(8,128)(2,1)}, u32[]{:S(2)}, u32[]{:S(2)}) collective-permute-start(bf16[4,512,256]{2,1,0:T(8,128)(2,1)} %code_pair.11), channel_id=1, source_target_pairs={{0,4},{2,6},{4,0},{6,2},{8,12},{10,14},{12,8},{14,10},{16,20},{18,... | collective-permute-start | bytes 3145736 | tf_op jit(solution)/shard_map/ppermute | solution.py:160
  185.0 65.6 %collective-permute-start.29 = (bf16[4,512,256]{2,1,0:T(8,128)(2,1)}, bf16[4,512,256]{2,1,0:T(8,128)(2,1)S(1)}, u32[]{:S(2)}, u32[]{:S(2)}) collective-permute-start(bf16[4,512,256]{2,1,0:T(8,128)(2,1)} %code_pair.13), channel_id=1, source_target_pairs={{0,4},{2,6},{4,0},{6,2},{8,12},{10,14},{12,8},{14,10},{16,20},{18,... | collective-permute-start | bytes 3145736 | tf_op jit(solution)/shard_map/ppermute | solution.py:160
  196.7 75.0 %collective-permute-start.38 = (bf16[4,512,256]{2,1,0:T(8,128)(2,1)}, bf16[4,512,256]{2,1,0:T(8,128)(2,1)}, u32[]{:S(2)}, u32[]{:S(2)}) collective-permute-start(bf16[4,512,256]{2,1,0:T(8,128)(2,1)} %code_pair.15), channel_id=1, source_target_pairs={{0,4},{2,6},{4,0},{6,2},{8,12},{10,14},{12,8},{14,10},{16,20},{18,... | collective-permute-start | bytes 3145736 | tf_op jit(solution)/shard_map/ppermute | solution.py:160
  278.4 42.6 %collective-permute-start.31 = (bf16[512,256]{1,0:T(8,128)(2,1)S(1)}, bf16[512,256]{1,0:T(8,128)(2,1)S(1)}, u32[]{:S(2)}, u32[]{:S(2)}) collective-permute-start(bf16[512,256]{1,0:T(8,128)(2,1)S(1)} %get-tuple-element.67), channel_id=1, source_target_pairs={{0,16},{2,18},{4,20},{6,22},{8,24},{10,26},{12,28},{14,30},{16,0},... | collective-permute-start | bytes 786440 | tf_op jit(solution)/shard_map/ppermute | solution.py:160
  279.4 48.9 %collective-permute-start.32 = (bf16[512,256]{1,0:T(8,128)(2,1)S(1)}, bf16[512,256]{1,0:T(8,128)(2,1)S(1)}, u32[]{:S(2)}, u32[]{:S(2)}) collective-permute-start(bf16[512,256]{1,0:T(8,128)(2,1)S(1)} %get-tuple-element.66), channel_id=1, source_target_pairs={{0,24},{2,26},{4,28},{6,30},{8,0},{10,2},{12,4},{14,6},{16,8},{18,... | collective-permute-start | bytes 786440 | tf_op jit(solution)/shard_map/ppermute | solution.py:160
  289.5 39.1 %collective-permute-start.39 = (bf16[512,256]{1,0:T(8,128)(2,1)S(1)}, bf16[512,256]{1,0:T(8,128)(2,1)S(1)}, u32[]{:S(2)}, u32[]{:S(2)}) collective-permute-start(bf16[512,256]{1,0:T(8,128)(2,1)S(1)} %get-tuple-element.54), channel_id=1, source_target_pairs={{0,8},{2,10},{4,12},{6,14},{8,16},{10,18},{12,20},{14,22},{16,24},... | collective-permute-start | bytes 786440 | tf_op jit(solution)/shard_map/ppermute | solution.py:160
  293.6 49.9 %collective-permute-start.40 = (bf16[512,256]{1,0:T(8,128)(2,1)S(1)}, bf16[512,256]{1,0:T(8,128)(2,1)S(1)}, u32[]{:S(2)}, u32[]{:S(2)}) collective-permute-start(bf16[512,256]{1,0:T(8,128)(2,1)S(1)} %get-tuple-element.56), channel_id=1, source_target_pairs={{0,16},{2,18},{4,20},{6,22},{8,24},{10,26},{12,28},{14,30},{16,0},... | collective-permute-start | bytes 786440 | tf_op jit(solution)/shard_map/ppermute | solution.py:160
  305.7 45.2 %collective-permute-start.41 = (bf16[512,256]{1,0:T(8,128)(2,1)S(1)}, bf16[512,256]{1,0:T(8,128)(2,1)S(1)}, u32[]{:S(2)}, u32[]{:S(2)}) collective-permute-start(bf16[512,256]{1,0:T(8,128)(2,1)S(1)} %get-tuple-element.55), channel_id=1, source_target_pairs={{0,24},{2,26},{4,28},{6,30},{8,0},{10,2},{12,4},{14,6},{16,8},{18,... | collective-permute-start | bytes 786440 | tf_op jit(solution)/shard_map/ppermute | solution.py:160
  328.3 43.3 %collective-permute-start.63 = (bf16[512,256]{1,0:T(8,128)(2,1)S(1)}, bf16[512,256]{1,0:T(8,128)(2,1)S(1)}, u32[]{:S(2)}, u32[]{:S(2)}) collective-permute-start(bf16[512,256]{1,0:T(8,128)(2,1)S(1)} %get-tuple-element.20), channel_id=1, source_target_pairs={{0,16},{2,18},{4,20},{6,22},{8,24},{10,26},{12,28},{14,30},{16,0},... | collective-permute-start | bytes 786440 | tf_op jit(solution)/shard_map/ppermute | solution.py:160
  328.6 43.1 %collective-permute-start.64 = (bf16[512,256]{1,0:T(8,128)(2,1)S(1)}, bf16[512,256]{1,0:T(8,128)(2,1)S(1)}, u32[]{:S(2)}, u32[]{:S(2)}) collective-permute-start(bf16[512,256]{1,0:T(8,128)(2,1)S(1)} %get-tuple-element.20), channel_id=1, source_target_pairs={{0,8},{2,10},{4,12},{6,14},{8,16},{10,18},{12,20},{14,22},{16,24},... | collective-permute-start | bytes 786440 | tf_op jit(solution)/shard_map/ppermute | solution.py:160
  350.9 43.2 %collective-permute-start.57 = (bf16[512,256]{1,0:T(8,128)(2,1)S(1)}, bf16[512,256]{1,0:T(8,128)(2,1)S(1)}, u32[]{:S(2)}, u32[]{:S(2)}) collective-permute-start(bf16[512,256]{1,0:T(8,128)(2,1)S(1)} %get-tuple-element.23), channel_id=1, source_target_pairs={{0,16},{2,18},{4,20},{6,22},{8,24},{10,26},{12,28},{14,30},{16,0},... | collective-permute-start | bytes 786440 | tf_op jit(solution)/shard_map/ppermute | solution.py:160
  351.6 42.5 %collective-permute-start.58 = (bf16[512,256]{1,0:T(8,128)(2,1)S(1)}, bf16[512,256]{1,0:T(8,128)(2,1)S(1)}, u32[]{:S(2)}, u32[]{:S(2)}) collective-permute-start(bf16[512,256]{1,0:T(8,128)(2,1)S(1)} %get-tuple-element.23), channel_id=1, source_target_pairs={{0,8},{2,10},{4,12},{6,14},{8,16},{10,18},{12,20},{14,22},{16,24},... | collective-permute-start | bytes 786440 | tf_op jit(solution)/shard_map/ppermute | solution.py:160
  371.8 44.8 %collective-permute-start.51 = (bf16[512,256]{1,0:T(8,128)(2,1)S(1)}, bf16[512,256]{1,0:T(8,128)(2,1)S(1)}, u32[]{:S(2)}, u32[]{:S(2)}) collective-permute-start(bf16[512,256]{1,0:T(8,128)(2,1)S(1)} %get-tuple-element.26), channel_id=1, source_target_pairs={{0,16},{2,18},{4,20},{6,22},{8,24},{10,26},{12,28},{14,30},{16,0},... | collective-permute-start | bytes 786440 | tf_op jit(solution)/shard_map/ppermute | solution.py:160
  373.4 44.7 %collective-permute-start.52 = (bf16[512,256]{1,0:T(8,128)(2,1)S(1)}, bf16[512,256]{1,0:T(8,128)(2,1)S(1)}, u32[]{:S(2)}, u32[]{:S(2)}) collective-permute-start(bf16[512,256]{1,0:T(8,128)(2,1)S(1)} %get-tuple-element.26), channel_id=1, source_target_pairs={{0,8},{2,10},{4,12},{6,14},{8,16},{10,18},{12,20},{14,22},{16,24},... | collective-permute-start | bytes 786440 | tf_op jit(solution)/shard_map/ppermute | solution.py:160
  427.3 47.1 %collective-permute-start.60 = (bf16[4,512,256]{2,1,0:T(8,128)(2,1)S(1)}, bf16[4,512,256]{2,1,0:T(8,128)(2,1)}, u32[]{:S(2)}, u32[]{:S(2)}) collective-permute-start(bf16[4,512,256]{2,1,0:T(8,128)(2,1)S(1)} %pad_maximum_fusion.8.refs_0_), channel_id=1, source_target_pairs={{0,4},{2,6},{4,0},{6,2},{8,12},{10,14},{12,8},{14,10},{16,20},{18,... | collective-permute-start | bytes 3145736 | tf_op jit(solution)/shard_map/ppermute | solution.py:160
  437.7 36.7 %collective-permute-start.65 = (bf16[4,512,256]{2,1,0:T(8,128)(2,1)S(1)}, bf16[4,512,256]{2,1,0:T(8,128)(2,1)S(1)}, u32[]{:S(2)}, u32[]{:S(2)}) collective-permute-start(bf16[4,512,256]{2,1,0:T(8,128)(2,1)S(1)} %pad_maximum_fusion.9.refs_0_), channel_id=1, source_target_pairs={{0,2},{2,0},{4,6},{6,4},{8,10},{10,8},{12,14},{14,12},{16,18},{18,... | collective-permute-start | bytes 3145736 | tf_op jit(solution)/shard_map/ppermute | solution.py:206
  437.7 59.1 %collective-permute-start.54 = (bf16[4,512,256]{2,1,0:T(8,128)(2,1)}, bf16[4,512,256]{2,1,0:T(8,128)(2,1)}, u32[]{:S(2)}, u32[]{:S(2)}) collective-permute-start(bf16[4,512,256]{2,1,0:T(8,128)(2,1)} %pad_maximum_fusion.7.refs_0_), channel_id=1, source_target_pairs={{0,4},{2,6},{4,0},{6,2},{8,12},{10,14},{12,8},{14,10},{16,20},{18,... | collective-permute-start | bytes 3145736 | tf_op jit(solution)/shard_map/ppermute | solution.py:160
  439.3 57.6 %collective-permute-start.59 = (bf16[4,512,256]{2,1,0:T(8,128)(2,1)S(1)}, bf16[4,512,256]{2,1,0:T(8,128)(2,1)S(1)}, u32[]{:S(2)}, u32[]{:S(2)}) collective-permute-start(bf16[4,512,256]{2,1,0:T(8,128)(2,1)S(1)} %pad_maximum_fusion.8.refs_0_), channel_id=1, source_target_pairs={{0,2},{2,0},{4,6},{6,4},{8,10},{10,8},{12,14},{14,12},{16,18},{18,... | collective-permute-start | bytes 3145736 | tf_op jit(solution)/shard_map/ppermute | solution.py:206
  451.8 64.7 %collective-permute-start.48 = (bf16[4,512,256]{2,1,0:T(8,128)(2,1)S(1)}, bf16[4,512,256]{2,1,0:T(8,128)(2,1)}, u32[]{:S(2)}, u32[]{:S(2)}) collective-permute-start(bf16[4,512,256]{2,1,0:T(8,128)(2,1)S(1)} %pad_maximum_fusion.6.refs_0_), channel_id=1, source_target_pairs={{0,4},{2,6},{4,0},{6,2},{8,12},{10,14},{12,8},{14,10},{16,20},{18,... | collective-permute-start | bytes 3145736 | tf_op jit(solution)/shard_map/ppermute | solution.py:160
  474.4 42.1 %collective-permute-start.67 = (bf16[4,512,256]{2,1,0:T(8,128)(2,1)S(1)}, bf16[4,512,256]{2,1,0:T(8,128)(2,1)S(1)}, u32[]{:S(2)}, u32[]{:S(2)}) collective-permute-start(bf16[4,512,256]{2,1,0:T(8,128)(2,1)S(1)} %collective-permute-done.66.refs_1_), channel_id=1, source_target_pairs={{0,2},{2,0},{4,6},{6,4},{8,10},{10,8},{12,14},{14,12},{16,18},{18,... | collective-permute-start | bytes 3145736 | tf_op jit(solution)/shard_map/ppermute | solution.py:206
  474.4 72.0 %collective-permute-start.53 = (bf16[4,512,256]{2,1,0:T(8,128)(2,1)}, bf16[4,512,256]{2,1,0:T(8,128)(2,1)}, u32[]{:S(2)}, u32[]{:S(2)}) collective-permute-start(bf16[4,512,256]{2,1,0:T(8,128)(2,1)} %pad_maximum_fusion.7.refs_0_), channel_id=1, source_target_pairs={{0,2},{2,0},{4,6},{6,4},{8,10},{10,8},{12,14},{14,12},{16,18},{18,... | collective-permute-start | bytes 3145736 | tf_op jit(solution)/shard_map/ppermute | solution.py:206
  496.9 53.8 %collective-permute-start.47 = (bf16[4,512,256]{2,1,0:T(8,128)(2,1)S(1)}, bf16[4,512,256]{2,1,0:T(8,128)(2,1)S(1)}, u32[]{:S(2)}, u32[]{:S(2)}) collective-permute-start(bf16[4,512,256]{2,1,0:T(8,128)(2,1)S(1)} %pad_maximum_fusion.6.refs_0_), channel_id=1, source_target_pairs={{0,2},{2,0},{4,6},{6,4},{8,10},{10,8},{12,14},{14,12},{16,18},{18,... | collective-permute-start | bytes 3145736 | tf_op jit(solution)/shard_map/ppermute | solution.py:206
  496.9 41.1 %collective-permute-start.61 = (bf16[4,512,256]{2,1,0:T(8,128)(2,1)}, bf16[4,512,256]{2,1,0:T(8,128)(2,1)}, u32[]{:S(2)}, u32[]{:S(2)}) collective-permute-start(bf16[4,512,256]{2,1,0:T(8,128)(2,1)} %collective-permute-done.60.refs_1_), channel_id=1, source_target_pairs={{0,2},{2,0},{4,6},{6,4},{8,10},{10,8},{12,14},{14,12},{16,18},{18,... | collective-permute-start | bytes 3145736 | tf_op jit(solution)/shard_map/ppermute | solution.py:206
  516.5 34.2 %collective-permute-start.49 = (bf16[4,512,256]{2,1,0:T(8,128)(2,1)}, bf16[4,512,256]{2,1,0:T(8,128)(2,1)S(1)}, u32[]{:S(2)}, u32[]{:S(2)}) collective-permute-start(bf16[4,512,256]{2,1,0:T(8,128)(2,1)} %collective-permute-done.48.refs_1_), channel_id=1, source_target_pairs={{0,2},{2,0},{4,6},{6,4},{8,10},{10,8},{12,14},{14,12},{16,18},{18,... | collective-permute-start | bytes 3145736 | tf_op jit(solution)/shard_map/ppermute | solution.py:206
  (74 other events, 1727.3 us)

commit v2 on v1

--- a/solution.py
+++ b/solution.py
@@ -13,18 +13,12 @@
 outer_rate = 0.7
 mix_share = 0.5
 
-RESIDUE = (
-    6.579736255284624,
-    -12.98787530573671,
-    12.207952703195676,
-    -6.691029741717024,
-    2.3803828656044055,
-    -0.5278879155971964,
-)
-
-CHUNKS = 4
+RESIDUE = (6.579735248418329, -12.987673932477895, 12.201508758913876, -6.6188575657590425, 2.0504529183602735)
+
+SHARES = (1, 1, 1, 1)
+CHUNKS = len(SHARES)
 TILE = 256
-STRIP = 16
+STRIP = 32
 MERGE_TILE = 256
 
 
@@ -46,8 +40,9 @@
     return f32((scaling * (smooth - offset)).astype(jnp.bfloat16))
 
 
-def code_kernel(where_ref, anchor_ref, *refs, strip, first):
-    slots, tile, width = anchor_ref.shape
+def code_kernel(where_ref, head_ref, rest_ref, *refs, strip, first):
+    slots, tile, width = rest_ref.shape
+    slots += 1
     own_refs, mate_refs = refs[:slots], refs[slots : 2 * slots]
     own_off, mate_off, out_ref, own_wide, mate_wide = refs[2 * slots :]
     per = width // BLOCK
@@ -64,7 +59,7 @@
         for s in range(slots):
             for b in range(per):
                 lanes = slice(b * BLOCK, (b + 1) * BLOCK)
-                anchor = f32(anchor_ref[s, rows, lanes])
+                anchor = f32(rest_ref[s - 1, rows, lanes] if s else head_ref[rows, lanes])
                 total = coded_strip(anchor, own_refs[s][rows, lanes], own_wide[s, rows, lanes])
                 total += coded_strip(anchor, mate_refs[s][rows, lanes], mate_wide[s, rows, lanes])
                 out_ref[s, rows, lanes] = total.astype(out_ref.dtype)
@@ -73,15 +68,19 @@
     lax.fori_loop(0, tile // strip, step, 0)
 
 
-def code(where, anchor, weights, mate, own_off, mate_off, group, row):
-    slots, rows, width = anchor.shape
+def code(where, head, rest, weights, mate, own_off, mate_off, group, row):
+    slots, rows, width = rest.shape
+    slots += 1
     half = weights.shape[0] // 2
-    tile = min(TILE, rows)
-    strip = min(STRIP, tile)
+    tile = math.gcd(rows, row, TILE)
+    strip = math.gcd(tile, STRIP)
     blocks = own_off.shape[1]
     row_of = lambda i, w: w[0] * (half // tile) + row // tile + i
     column = lambda s: 1 + group * slots + s
-    in_specs = [pl.BlockSpec((slots, tile, width), lambda i, w: (0, i, 0))]
+    in_specs = [
+        pl.BlockSpec((tile, width), lambda i, w: (row // tile + i, 0)),
+        pl.BlockSpec((slots - 1, tile, width), lambda i, w: (0, i, 0)),
+    ]
     in_specs += [pl.BlockSpec((tile, width), lambda i, w, s=s: (row_of(i, w), w[column(s)])) for s in range(slots)]
     in_specs += [pl.BlockSpec((tile, width), lambda i, w, s=s: (i, w[column(s)])) for s in range(slots)]
     in_specs += [
@@ -90,7 +89,7 @@
     ]
     return pl.pallas_call(
         functools.partial(code_kernel, strip=strip, first=group * slots * (width // BLOCK)),
-        out_shape=jax.ShapeDtypeStruct(anchor.shape, jnp.bfloat16),
+        out_shape=jax.ShapeDtypeStruct((slots, rows, width), jnp.bfloat16),
         grid_spec=pltpu.PrefetchScalarGridSpec(
             num_scalar_prefetch=1,
             grid=(rows // tile,),
@@ -100,8 +99,10 @@
         ),
         name="code_pair",
         compiler_params=pltpu.CompilerParams(dimension_semantics=("arbitrary",)),
-        cost_estimate=pl.CostEstimate(flops=80 * anchor.size, transcendentals=0, bytes_accessed=8 * anchor.size),
-    )(where, anchor, *([weights] * slots), *([mate] * slots), own_off, mate_off)
+        cost_estimate=pl.CostEstimate(
+            flops=80 * slots * rows * width, transcendentals=0, bytes_accessed=8 * slots * rows * width
+        ),
+    )(where, head, rest, *([weights] * slots), *([mate] * slots), own_off, mate_off)
 
 
 def merge_kernel(where_ref, *refs, groups):
@@ -117,7 +118,7 @@
 def merge(where, fresh, weights, row, mine, so_far):
     slots, rows, width = fresh[0].shape
     half = weights.shape[0] // 2
-    tile = min(MERGE_TILE, rows)
+    tile = math.gcd(rows, row, MERGE_TILE)
 
     def place(i, w):
         return ((w[0] if mine else 1 - w[0]) * (half // tile) + row // tile + i, 0)
@@ -181,10 +182,8 @@
 
     gathered = [columns(place)] + [shifted(columns(place + s), s) for s in range(1, share)]
     partial = jnp.dot(jnp.concatenate(gathered), weights, preferred_element_type=jnp.float32)
-    total = partial[:tokens]
-    for s in range(1, share):
-        total += shifted(partial[s * tokens : (s + 1) * tokens], -s)
-    return total.astype(jnp.bfloat16)
+    parts = [partial[:tokens]] + [shifted(partial[s * tokens : (s + 1) * tokens], -s) for s in range(1, share)]
+    return sum(parts[1:], parts[0]).astype(jnp.bfloat16)
 
 
 def shards(hidden, local_weight, master, momentum, dither):
@@ -198,7 +197,6 @@
     x_line = Line(replicas, x_length, 2)
     z_line = Line(replicas, z_length, 2 * x_length)
     half = rows // 2
-    piece = half // CHUNKS
     width = columns // chips
     mine, theirs = core * half, (1 - core) * half
 
@@ -211,14 +209,17 @@
     def beside(own, other):
         return jnp.where(core == 0, jnp.concatenate([own, other], 1), jnp.concatenate([other, own], 1))
 
-    rounded = master.astype(jnp.bfloat16)
-    anchor = beside(halves(rounded, mine), swap(halves(rounded, theirs)))
-    parts = [slice(i * piece, (i + 1) * piece) for i in range(CHUNKS)]
-
-    groups = []
+    edges = [half * sum(SHARES[:i]) // sum(SHARES) for i in range(CHUNKS + 1)]
+    parts = [slice(a, b) for a, b in zip(edges, edges[1:])]
+
+    rounded = [halves(master, start).astype(jnp.bfloat16) for start in (mine, theirs)]
+    anchor = beside(rounded[0], swap(rounded[1]))
+
+    heads = x_line.gather(anchor)
+    rests = []
     for part in parts:
         pieces = z_line.gather(anchor[part])
-        groups.append(x_line.gather(jnp.stack(pieces)))
+        rests.append(x_line.gather(jnp.stack(pieces[1:])))
 
     d = jnp.arange(z_length, dtype=jnp.int32)[None, :]
     e = jnp.arange(x_length, dtype=jnp.int32)[:, None]
@@ -231,7 +232,7 @@
     offset = jnp.dot(offset.astype(jnp.bfloat16), pick.astype(jnp.bfloat16), preferred_element_type=jnp.float32)
     offset = offset.astype(jnp.bfloat16)
     mate_offset = swap(halves(offset, theirs))
-    mates = [swap(halves(weights, theirs + i * piece, piece)) for i in range(CHUNKS)]
+    mates = [swap(halves(weights, theirs + part.start, part.stop - part.start)) for part in parts]
     pair_master = beside(halves(master, mine), swap(halves(master, theirs)))
     pair_momentum = beside(halves(momentum, mine), swap(halves(momentum, theirs)))
     key_values = project(hidden, weights)
@@ -240,17 +241,23 @@
     for i, part in enumerate(parts):
         sums = [None] * x_length
         for g in reversed(range(x_length)):
-            sums[g] = code(where, groups[i][g], weights, mates[i], offset, mate_offset, g, i * piece)
-        summed = x_line.reduce(sums).astype(jnp.bfloat16)
-        averaged = z_line.reduce([summed[k] for k in range(z_length)]) / replicas
+            sums[g] = code(where, heads[g], rests[i][g], weights, mates[i], offset, mate_offset, g, part.start)
+        arrived = [x_line.send(sums[e], e) for e in range(1, x_length)]
+        summed = [
+            sum((f32(a[k]) for a in arrived), f32(sums[0][k])).astype(jnp.bfloat16) for k in range(z_length)
+        ]
+        total = z_line.reduce(summed)
         old_master, old_momentum, *_ = lax.optimization_barrier((pair_master[part], pair_momentum[part], *masters[-1:]))
+        averaged = total / replicas
         new_momentum = momentum_keep * old_momentum + averaged
         new_master = old_master - outer_rate * (averaged + momentum_keep * new_momentum)
         masters.append(new_master)
         momenta.append(new_momentum)
         pieces = z_line.gather(new_master.astype(jnp.bfloat16))
         fresh.append(x_line.gather(jnp.stack(pieces)))
-        swapped.append([swap(group) for group in fresh[-1]])
+        swapped.append([None] * x_length)
+        for g, group in enumerate(fresh[-1]):
+            swapped[-1][g] = swap(group)
 
     def home(pieces):
         pair = jnp.concatenate(pieces)
@@ -262,11 +269,9 @@
 
     final_master, final_momentum = home(masters), home(momenta)
     new_local = None
-    for i in range(CHUNKS + 1):
-        if i < CHUNKS:
-            new_local = merge(where, fresh[i], weights, i * piece, True, new_local)
-        if i > 0:
-            new_local = merge(where, swapped[i - 1], weights, (i - 1) * piece, False, new_local)
+    for i, part in enumerate(parts):
+        new_local = merge(where, fresh[i], weights, part.start, True, new_local)
+        new_local = merge(where, swapped[i], weights, part.start, False, new_local)
     return (key_values, final_master, final_momentum, new_local[None])
 
 

time: 558 us -> 566 us (1.014)
  waiting for transfers between devices: 203 us -> 277 us
  starting transfers between devices: 172 us -> 137 us
  Pallas kernels: 119 us -> 104 us
  local copies, waits for them, and re-layouts: 23.9 us -> 14.8 us
  matrix products: 13.8 us -> 6.43 us
    ppermute x48 -> x49, waiting for transfers between devices: 185 us -> 264 us  [send(): lax.ppermute(array, 'rep', [(i, target(i)) for i in range(self.total)])]
    ppermute x48 -> x49, starting transfers between devices: 165 us -> 131 us  [send(): lax.ppermute(array, 'rep', [(i, target(i)) for i in range(self.total)])]
    pallas_call x8, Pallas kernels: 85.3 us -> 70.4 us  [code(): pl.pallas_call(functools.partial(code_kernel, strip=strip, first=group *...]
    dot_general x1, matrix products: 12.4 us -> 5.94 us  [project(): jnp.dot(jnp.concatenate(gathered), weights, preferred_element_type=jnp.fl...]
  transfers between devices with their start and end apart: 68 -> 69, of which waited for: 25 -> 24; matrix products, arithmetic and copies ran while one was open for 10% -> 7% of each run, Pallas kernels for 21% -> 18%
where the time goes in v2:
time: 566 us
  waiting for transfers between devices  277 us (49%)
  starting transfers between devices  137 us (24%)
  Pallas kernels  104 us (18%)
  other arithmetic  25.3 us (4%)
  local copies, waits for them, and re-layouts  14.8 us (3%)
  matrix products  6.43 us (1%)
    ppermute x49, waiting for transfers between devices, send(): lax.ppermute(array, 'rep', [(i, target(i)) for i in range(self.total)])  264 us
    ppermute x49, starting transfers between devices, send(): lax.ppermute(array, 'rep', [(i, target(i)) for i in range(self.total)])  131 us
    pallas_call x8, Pallas kernels, code(): pl.pallas_call(functools.partial(code_kernel, strip=strip, first=group *...  70.4 us
    pallas_call x8, Pallas kernels, merge(): pl.pallas_call(functools.partial(merge_kernel, groups=len(fresh)), out_sh...  33.9 us
    ppermute x2, waiting for transfers between devices, shifted(): lax.ppermute(array, 'fsdp', [(i, (i + by) % share) for i in range(share)])  12.1 us
  transfers between devices with their start and end apart: 69, of which 24 were waited for; matrix products, arithmetic and copies ran while one was open for 7% of the time, Pallas kernels for 18%

profile of v2, /device:TPU:0, one launch (start us, length us, event | category | flops | bytes accessed | tf_op | source)
XLA Modules:
  0.0 565.5 jit_solution(10150009388850412212)
XLA Ops:
  19.9 8.0 %dynamic-slice_bitcast_fusion = (bf16[512,2048]{1,0:T(8,128)(2,1)}, bf16[512,2048]{1,0:T(8,128)(2,1)}, bf16[512,2048]{1,0:T(8,128)(2,1)}, bf16[512,2048]{1,0:T(8,128)(2,1)}) fusion(bf16[1,4096,2048]{2,1,0:T(8,128)(2,1)} %param.6, s32[]{:T(128)S(6)} %select_n.150, s32[]{:T(128)S(6)} %select_n.148, s32[]{:T(128)S(6)} %select_n.138, s32[]{:T(128)S(6)} %select_n.149), kind=kLoop, calls=%fused_computation.11 | loop fusion | bytes 16777232 | tf_op jit(solution)/shard_map/dynamic_slice | solution.py:207
  28.0 8.2 %collective-permute-done.6 = bf16[512,256]{1,0:T(8,128)(2,1)S(1)} collective-permute-done((bf16[512,256]{1,0:T(8,128)(2,1)}, bf16[512,256]{1,0:T(8,128)(2,1)S(1)}, u32[]{:S(2)}, u32[]{:S(2)}) %collective-permute-start.6) | collective-permute-done | bytes 262176 | tf_op jit(solution)/shard_map/ppermute | solution.py:161
  40.1 17.9 %collective-permute-done.17 = bf16[512,256]{1,0:T(8,128)(2,1)S(1)} collective-permute-done((bf16[512,256]{1,0:T(8,128)(2,1)}, bf16[512,256]{1,0:T(8,128)(2,1)S(1)}, u32[]{:S(2)}, u32[]{:S(2)}) %collective-permute-start.17) | collective-permute-done | bytes 262176 | tf_op jit(solution)/shard_map/ppermute | solution.py:161
  58.1 12.2 %collective-permute-start.27 = (bf16[512,256]{1,0:T(8,128)(2,1)}, bf16[512,256]{1,0:T(8,128)(2,1)S(1)}, u32[]{:S(2)}, u32[]{:S(2)}) collective-permute-start(bf16[512,256]{1,0:T(8,128)(2,1)} %get-tuple-element.71), channel_id=1, source_target_pairs={{0,8},{2,10},{4,12},{6,14},{8,16},{10,18},{12,20},{14,22},{16,24},... | collective-permute-start | bytes 786440 | tf_op jit(solution)/shard_map/ppermute | solution.py:161
  79.9 9.0 %collective-permute-start.35 = (bf16[512,256]{1,0:T(8,128)(2,1)S(1)}, bf16[512,256]{1,0:T(8,128)(2,1)S(1)}, u32[]{:S(2)}, u32[]{:S(2)}) collective-permute-start(bf16[512,256]{1,0:T(8,128)(2,1)S(1)} %copy-done.39), channel_id=1, source_target_pairs={{0,16},{2,18},{4,20},{6,22},{8,24},{10,26},{12,28},{14,30},{16,0},... | collective-permute-start | bytes 786440 | tf_op jit(solution)/shard_map/ppermute | solution.py:161
  90.6 10.5 %collective-permute-done.35 = bf16[512,256]{1,0:T(8,128)(2,1)S(1)} collective-permute-done((bf16[512,256]{1,0:T(8,128)(2,1)S(1)}, bf16[512,256]{1,0:T(8,128)(2,1)S(1)}, u32[]{:S(2)}, u32[]{:S(2)}) %collective-permute-start.35) | collective-permute-done | bytes 262176 | tf_op jit(solution)/shard_map/ppermute | solution.py:161
  101.7 9.2 %collective-permute-done.36 = bf16[512,256]{1,0:T(8,128)(2,1)S(1)} collective-permute-done((bf16[512,256]{1,0:T(8,128)(2,1)S(1)}, bf16[512,256]{1,0:T(8,128)(2,1)S(1)}, u32[]{:S(2)}, u32[]{:S(2)}) %collective-permute-start.36) | collective-permute-done | bytes 262176 | tf_op jit(solution)/shard_map/ppermute | solution.py:161
  117.9 19.1 %collective-permute-done.10.head_ref = bf16[2048,256]{1,0:T(8,128)(2,1)S(1)} collective-permute-done((bf16[2048,256]{1,0:T(8,128)(2,1)S(1)}, bf16[2048,256]{1,0:T(8,128)(2,1)S(1)}, u32[]{:S(2)}, u32[]{:S(2)}) %collective-permute-start.10) | collective-permute-done | bytes 1048608 | tf_op jit(solution)/shard_map/ppermute | solution.py:161
  137.0 14.9 %collective-permute-done.20.rest_ref = bf16[3,512,256]{2,1,0:T(8,128)(2,1)S(1)} collective-permute-done((bf16[3,512,256]{2,1,0:T(8,128)(2,1)S(1)}, bf16[3,512,256]{2,1,0:T(8,128)(2,1)S(1)}, u32[]{:S(2)}, u32[]{:S(2)}) %collective-permute-start.20) | collective-permute-done | bytes 786464 | tf_op jit(solution)/shard_map/ppermute | solution.py:161
  159.5 8.9 %code_pair.9 = bf16[4,512,256]{2,1,0:T(8,128)(2,1)} custom-call(s32[9]{0:T(128)} %pad_add_fusion.where_ref, bf16[2048,256]{1,0:T(8,128)(2,1)} %copy-done.5, bf16[3,512,256]{2,1,0:T(8,128)(2,1)} %copy-done.33, bf16[4096,2048]{1,0:T(8,128)(2,1)} %bitcast.108, bf16[4096,2048]{1,0:T(8,128)(2,1)} %bitcast.109, bf16[4096,2048]{1,0:T(8,128)(2,1)} %bitcast.110, ...), custom_call_target="tpu_custom_call" | custom-call | flops 41943040 | bytes 4194304 | tf_op jit(solution)/shard_map/code_pair/pallas_call | solution.py:90
  175.9 8.8 %code_pair.11 = bf16[4,512,256]{2,1,0:T(8,128)(2,1)} custom-call(s32[9]{0:T(128)} %pad_add_fusion.where_ref, bf16[2048,256]{1,0:T(8,128)(2,1)} %copy-done.5, bf16[3,512,256]{2,1,0:T(8,128)(2,1)} %copy-done.34, bf16[4096,2048]{1,0:T(8,128)(2,1)} %bitcast.112, bf16[4096,2048]{1,0:T(8,128)(2,1)} %bitcast.113, bf16[4096,2048]{1,0:T(8,128)(2,1)} %bitcast.114, ...), custom_call_target="tpu_custom_call" | custom-call | flops 41943040 | bytes 4194304 | tf_op jit(solution)/shard_map/code_pair/pallas_call | solution.py:90
  187.6 8.9 %code_pair.13 = bf16[4,512,256]{2,1,0:T(8,128)(2,1)} custom-call(s32[9]{0:T(128)} %pad_add_fusion.where_ref, bf16[2048,256]{1,0:T(8,128)(2,1)} %copy-done.5, bf16[3,512,256]{2,1,0:T(8,128)(2,1)} %copy-done.35, bf16[4096,2048]{1,0:T(8,128)(2,1)} %bitcast.116, bf16[4096,2048]{1,0:T(8,128)(2,1)} %bitcast.117, bf16[4096,2048]{1,0:T(8,128)(2,1)} %bitcast.118, ...), custom_call_target="tpu_custom_call" | custom-call | flops 41943040 | bytes 4194304 | tf_op jit(solution)/shard_map/code_pair/pallas_call | solution.py:90
  198.8 8.8 %code_pair.15 = bf16[4,512,256]{2,1,0:T(8,128)(2,1)} custom-call(s32[9]{0:T(128)} %pad_add_fusion.where_ref, bf16[2048,256]{1,0:T(8,128)(2,1)} %copy-done.5, bf16[3,512,256]{2,1,0:T(8,128)(2,1)} %collective-permute-done.38.rest_ref, bf16[4096,2048]{1,0:T(8,128)(2,1)} %bitcast.120, bf16[4096,2048]{1,0:T(8,128)(2,1)} %bitcast.121, ...), custom_call_target="tpu_custom_call" | custom-call | flops 41943040 | bytes 4194304 | tf_op jit(solution)/shard_map/code_pair/pallas_call | solution.py:90
  211.4 8.7 %code_pair.8 = bf16[4,512,256]{2,1,0:T(8,128)(2,1)} custom-call(s32[9]{0:T(128)} %pad_add_fusion.where_ref, bf16[2048,256]{1,0:T(8,128)(2,1)} %copy-done.2, bf16[3,512,256]{2,1,0:T(8,128)(2,1)} %copy-done.16, bf16[4096,2048]{1,0:T(8,128)(2,1)} %bitcast.126, bf16[4096,2048]{1,0:T(8,128)(2,1)} %bitcast.125, bf16[4096,2048]{1,0:T(8,128)(2,1)} %bitcast.124, ...), custom_call_target="tpu_custom_call" | custom-call | flops 41943040 | bytes 4194304 | tf_op jit(solution)/shard_map/code_pair/pallas_call | solution.py:90
  220.1 8.8 %code_pair.10 = bf16[4,512,256]{2,1,0:T(8,128)(2,1)} custom-call(s32[9]{0:T(128)} %pad_add_fusion.where_ref, bf16[2048,256]{1,0:T(8,128)(2,1)} %copy-done.2, bf16[3,512,256]{2,1,0:T(8,128)(2,1)} %copy-done.17, bf16[4096,2048]{1,0:T(8,128)(2,1)} %bitcast.128, bf16[4096,2048]{1,0:T(8,128)(2,1)} %bitcast.129, bf16[4096,2048]{1,0:T(8,128)(2,1)} %bitcast.130, ...), custom_call_target="tpu_custom_call" | custom-call | flops 41943040 | bytes 4194304 | tf_op jit(solution)/shard_map/code_pair/pallas_call | solution.py:90
  228.9 8.8 %code_pair.12 = bf16[4,512,256]{2,1,0:T(8,128)(2,1)} custom-call(s32[9]{0:T(128)} %pad_add_fusion.where_ref, bf16[2048,256]{1,0:T(8,128)(2,1)} %copy-done.2, bf16[3,512,256]{2,1,0:T(8,128)(2,1)} %pad_maximum_fusion.8.rest_ref, bf16[4096,2048]{1,0:T(8,128)(2,1)} %bitcast.132, bf16[4096,2048]{1,0:T(8,128)(2,1)} %bitcast.133, bf16[4096,2048]{1,0:T(8,128)(2,1)} %bitcast.134, ...), custom_call_target="tpu_custom_call" | custom-call | flops 41943040 | bytes 4194304 | tf_op jit(solution)/shard_map/code_pair/pallas_call | solution.py:90
  237.7 8.9 %code_pair.14 = bf16[4,512,256]{2,1,0:T(8,128)(2,1)} custom-call(s32[9]{0:T(128)} %pad_add_fusion.where_ref, bf16[2048,256]{1,0:T(8,128)(2,1)} %copy-done.2, bf16[3,512,256]{2,1,0:T(8,128)(2,1)} %pad_maximum_fusion.9.rest_ref, bf16[4096,2048]{1,0:T(8,128)(2,1)} %bitcast.136, bf16[4096,2048]{1,0:T(8,128)(2,1)} %bitcast.137, bf16[4096,2048]{1,0:T(8,128)(2,1)} %bitcast.138, ...), custom_call_target="tpu_custom_call" | custom-call | flops 41943040 | bytes 4194304 | tf_op jit(solution)/shard_map/code_pair/pallas_call | solution.py:90
  261.7 19.7 %collective-permute-done.39 = bf16[4,512,256]{2,1,0:T(8,128)(2,1)} collective-permute-done((bf16[4,512,256]{2,1,0:T(8,128)(2,1)}, bf16[4,512,256]{2,1,0:T(8,128)(2,1)}, u32[]{:S(2)}, u32[]{:S(2)}) %collective-permute-start.39) | collective-permute-done | bytes 1048608 | tf_op jit(solution)/shard_map/ppermute | solution.py:161
  303.3 8.8 %collective-permute-start.41 = (bf16[512,256]{1,0:T(8,128)(2,1)S(1)}, bf16[512,256]{1,0:T(8,128)(2,1)S(1)}, u32[]{:S(2)}, u32[]{:S(2)}) collective-permute-start(bf16[512,256]{1,0:T(8,128)(2,1)S(1)} %get-tuple-element.46), channel_id=1, source_target_pairs={{0,16},{2,18},{4,20},{6,22},{8,24},{10,26},{12,28},{14,30},{16,0},... | collective-permute-start | bytes 786440 | tf_op jit(solution)/shard_map/ppermute | solution.py:161
  317.2 10.6 %collective-permute-done.32 = bf16[512,256]{1,0:T(8,128)(2,1)S(1)} collective-permute-done((bf16[512,256]{1,0:T(8,128)(2,1)S(1)}, bf16[512,256]{1,0:T(8,128)(2,1)S(1)}, u32[]{:S(2)}, u32[]{:S(2)}) %collective-permute-start.32) | collective-permute-done | bytes 262176 | tf_op jit(solution)/shard_map/ppermute | solution.py:161
  327.8 7.6 %collective-permute-start.63 = (bf16[512,256]{1,0:T(8,128)(2,1)S(1)}, bf16[512,256]{1,0:T(8,128)(2,1)S(1)}, u32[]{:S(2)}, u32[]{:S(2)}) collective-permute-start(bf16[512,256]{1,0:T(8,128)(2,1)S(1)} %get-tuple-element.20), channel_id=1, source_target_pairs={{0,24},{2,26},{4,28},{6,30},{8,0},{10,2},{12,4},{14,6},{16,8},{18,... | collective-permute-start | bytes 786440 | tf_op jit(solution)/shard_map/ppermute | solution.py:161
  336.7 12.7 %collective-permute-start.65 = (bf16[512,256]{1,0:T(8,128)(2,1)S(1)}, bf16[512,256]{1,0:T(8,128)(2,1)S(1)}, u32[]{:S(2)}, u32[]{:S(2)}) collective-permute-start(bf16[512,256]{1,0:T(8,128)(2,1)S(1)} %get-tuple-element.20), channel_id=1, source_target_pairs={{0,8},{2,10},{4,12},{6,14},{8,16},{10,18},{12,20},{14,22},{16,24},... | collective-permute-start | bytes 786440 | tf_op jit(solution)/shard_map/ppermute | solution.py:161
  349.5 8.5 %collective-permute-start.57 = (bf16[512,256]{1,0:T(8,128)(2,1)S(1)}, bf16[512,256]{1,0:T(8,128)(2,1)S(1)}, u32[]{:S(2)}, u32[]{:S(2)}) collective-permute-start(bf16[512,256]{1,0:T(8,128)(2,1)S(1)} %get-tuple-element.22), channel_id=1, source_target_pairs={{0,24},{2,26},{4,28},{6,30},{8,0},{10,2},{12,4},{14,6},{16,8},{18,... | collective-permute-start | bytes 786440 | tf_op jit(solution)/shard_map/ppermute | solution.py:161
  362.1 16.3 %collective-permute-done.64 = bf16[512,256]{1,0:T(8,128)(2,1)S(1)} collective-permute-done((bf16[512,256]{1,0:T(8,128)(2,1)S(1)}, bf16[512,256]{1,0:T(8,128)(2,1)S(1)}, u32[]{:S(2)}, u32[]{:S(2)}) %collective-permute-start.64) | collective-permute-done | bytes 262176 | tf_op jit(solution)/shard_map/ppermute | solution.py:161
  384.6 16.3 %collective-permute-done.58 = bf16[512,256]{1,0:T(8,128)(2,1)S(1)} collective-permute-done((bf16[512,256]{1,0:T(8,128)(2,1)S(1)}, bf16[512,256]{1,0:T(8,128)(2,1)S(1)}, u32[]{:S(2)}, u32[]{:S(2)}) %collective-permute-start.58) | collective-permute-done | bytes 262176 | tf_op jit(solution)/shard_map/ppermute | solution.py:161
  407.4 16.0 %collective-permute-done.52 = bf16[512,256]{1,0:T(8,128)(2,1)S(1)} collective-permute-done((bf16[512,256]{1,0:T(8,128)(2,1)S(1)}, bf16[512,256]{1,0:T(8,128)(2,1)S(1)}, u32[]{:S(2)}, u32[]{:S(2)}) %collective-permute-start.52) | collective-permute-done | bytes 262176 | tf_op jit(solution)/shard_map/ppermute | solution.py:161
  425.4 9.1 %collective-permute-done.46 = bf16[512,256]{1,0:T(8,128)(2,1)S(1)} collective-permute-done((bf16[512,256]{1,0:T(8,128)(2,1)S(1)}, bf16[512,256]{1,0:T(8,128)(2,1)S(1)}, u32[]{:S(2)}, u32[]{:S(2)}) %collective-permute-start.46) | collective-permute-done | bytes 262176 | tf_op jit(solution)/shard_map/ppermute | solution.py:161
  436.5 12.1 %collective-permute-done.1 = f32[128,2048]{1,0:T(8,128)S(1)} collective-permute-done((f32[128,2048]{1,0:T(8,128)}, f32[128,2048]{1,0:T(8,128)S(1)}, u32[]{:S(2)}, u32[]{:S(2)}) %collective-permute-start.1) | collective-permute-done | bytes 1048608 | tf_op jit(solution)/shard_map/ppermute | solution.py:181
  450.7 9.9 %collective-permute-done.67.refs_1_ = bf16[4,512,256]{2,1,0:T(8,128)(2,1)S(1)} collective-permute-done((bf16[4,512,256]{2,1,0:T(8,128)(2,1)S(1)}, bf16[4,512,256]{2,1,0:T(8,128)(2,1)S(1)}, u32[]{:S(2)}, u32[]{:S(2)}) %collective-permute-start.67) | collective-permute-done | bytes 1048608 | tf_op jit(solution)/shard_map/ppermute | solution.py:161
  462.0 21.1 %collective-permute-done.61.refs_1_ = bf16[4,512,256]{2,1,0:T(8,128)(2,1)} collective-permute-done((bf16[4,512,256]{2,1,0:T(8,128)(2,1)S(1)}, bf16[4,512,256]{2,1,0:T(8,128)(2,1)}, u32[]{:S(2)}, u32[]{:S(2)}) %collective-permute-start.61) | collective-permute-done | bytes 1048608 | tf_op jit(solution)/shard_map/ppermute | solution.py:161
  483.6 22.0 %collective-permute-done.55.refs_1_ = bf16[4,512,256]{2,1,0:T(8,128)(2,1)} collective-permute-done((bf16[4,512,256]{2,1,0:T(8,128)(2,1)S(1)}, bf16[4,512,256]{2,1,0:T(8,128)(2,1)}, u32[]{:S(2)}, u32[]{:S(2)}) %collective-permute-start.55) | collective-permute-done | bytes 1048608 | tf_op jit(solution)/shard_map/ppermute | solution.py:161
  505.6 21.5 %collective-permute-done.49.refs_1_ = bf16[4,512,256]{2,1,0:T(8,128)(2,1)} collective-permute-done((bf16[4,512,256]{2,1,0:T(8,128)(2,1)S(1)}, bf16[4,512,256]{2,1,0:T(8,128)(2,1)}, u32[]{:S(2)}, u32[]{:S(2)}) %collective-permute-start.49) | collective-permute-done | bytes 1048608 | tf_op jit(solution)/shard_map/ppermute | solution.py:161
  (255 shorter events, 172.6 us)
Async XLA Ops:
  16.0 42.0 %collective-permute-start.17 = (bf16[512,256]{1,0:T(8,128)(2,1)}, bf16[512,256]{1,0:T(8,128)(2,1)S(1)}, u32[]{:S(2)}, u32[]{:S(2)}) collective-permute-start(bf16[512,256]{1,0:T(8,128)(2,1)} %get-tuple-element.72), channel_id=1, source_target_pairs={{0,16},{2,18},{4,20},{6,22},{8,24},{10,26},{12,28},{14,30},{16,0},... | collective-permute-start | bytes 786440 | tf_op jit(solution)/shard_map/ppermute | solution.py:161
  19.0 39.1 %collective-permute-start.18 = (bf16[512,256]{1,0:T(8,128)(2,1)}, bf16[512,256]{1,0:T(8,128)(2,1)S(1)}, u32[]{:S(2)}, u32[]{:S(2)}) collective-permute-start(bf16[512,256]{1,0:T(8,128)(2,1)} %get-tuple-element.72), channel_id=1, source_target_pairs={{0,8},{2,10},{4,12},{6,14},{8,16},{10,18},{12,20},{14,22},{16,24},... | collective-permute-start | bytes 786440 | tf_op jit(solution)/shard_map/ppermute | solution.py:161
  36.2 115.8 %collective-permute-start.8 = (bf16[512,2048]{1,0:T(8,128)(2,1)}, bf16[512,2048]{1,0:T(8,128)(2,1)S(1)}, u32[]{:S(2)}, u32[]{:S(2)}) collective-permute-start(bf16[512,2048]{1,0:T(8,128)(2,1)} %get-tuple-element.34), channel_id=1, source_target_pairs={{0,2},{2,0},{4,6},{6,4},{8,10},{10,8},{12,14},{14,12},{16,18},{18,... | collective-permute-start | bytes 6291464 | tf_op jit(solution)/shard_map/ppermute | solution.py:204
  36.2 76.4 %collective-permute-start.2 = (f32[2048,128]{1,0:T(8,128)S(1)}, f32[2048,128]{1,0:T(8,128)S(1)}, u32[]{:S(2)}, u32[]{:S(2)}) collective-permute-start(f32[2048,128]{1,0:T(8,128)S(1)} %get-tuple-element.67), channel_id=1, source_target_pairs={{0,2},{2,0},{4,6},{6,4},{8,10},{10,8},{12,14},{14,12},{16,18},{18,... | collective-permute-start | bytes 3145736 | tf_op jit(solution)/shard_map/ppermute | solution.py:204
  70.5 42.7 %collective-permute-start = (bf16[128,4096]{1,0:T(8,128)(2,1)S(1)}, bf16[128,4096]{1,0:T(8,128)(2,1)S(1)}, u32[]{:S(2)}, u32[]{:S(2)}) collective-permute-start(bf16[128,4096]{1,0:T(8,128)(2,1)S(1)} %get-tuple-element.69), channel_id=1, source_target_pairs={{0,1},{1,0},{2,3},{3,2},{4,5},{5,4},{6,7},{7,6},{8,9},{9,8},{10,11... | collective-permute-start | bytes 3145736 | tf_op jit(solution)/shard_map/ppermute | solution.py:181
  112.6 39.4 %collective-permute-start.20 = (bf16[3,512,256]{2,1,0:T(8,128)(2,1)S(1)}, bf16[3,512,256]{2,1,0:T(8,128)(2,1)S(1)}, u32[]{:S(2)}, u32[]{:S(2)}) collective-permute-start(bf16[3,512,256]{2,1,0:T(8,128)(2,1)S(1)} %pad_maximum_fusion.7.rest_ref), channel_id=1, source_target_pairs={{0,4},{2,6},{4,0},{6,2},{8,12},{10,14},{12,8},{14,10},{16,20},{18,... | collective-permute-start | bytes 2359304 | tf_op jit(solution)/shard_map/ppermute | solution.py:161
  113.2 60.4 %collective-permute-start.19 = (bf16[512,2048]{1,0:T(8,128)(2,1)}, bf16[512,2048]{1,0:T(8,128)(2,1)}, u32[]{:S(2)}, u32[]{:S(2)}) collective-permute-start(bf16[512,2048]{1,0:T(8,128)(2,1)} %get-tuple-element.33), channel_id=1, source_target_pairs={{0,2},{2,0},{4,6},{6,4},{8,10},{10,8},{12,14},{14,12},{16,18},{18,... | collective-permute-start | bytes 6291464 | tf_op jit(solution)/shard_map/ppermute | solution.py:204
  113.8 70.8 %collective-permute-start.28 = (bf16[512,2048]{1,0:T(8,128)(2,1)}, bf16[512,2048]{1,0:T(8,128)(2,1)}, u32[]{:S(2)}, u32[]{:S(2)}) collective-permute-start(bf16[512,2048]{1,0:T(8,128)(2,1)} %get-tuple-element.35), channel_id=1, source_target_pairs={{0,2},{2,0},{4,6},{6,4},{8,10},{10,8},{12,14},{14,12},{16,18},{18,... | collective-permute-start | bytes 6291464 | tf_op jit(solution)/shard_map/ppermute | solution.py:204
  137.0 59.4 %collective-permute-start.3 = (f32[2048,128]{1,0:T(8,128)}, f32[2048,128]{1,0:T(8,128)}, u32[]{:S(2)}, u32[]{:S(2)}) collective-permute-start(f32[2048,128]{1,0:T(8,128)} %get-tuple-element.65), channel_id=1, source_target_pairs={{0,2},{2,0},{4,6},{6,4},{8,10},{10,8},{12,14},{14,12},{16,18},{18,... | collective-permute-start | bytes 3145736 | tf_op jit(solution)/shard_map/ppermute | solution.py:204
  151.9 46.8 %collective-permute-start.37 = (bf16[512,2048]{1,0:T(8,128)(2,1)}, bf16[512,2048]{1,0:T(8,128)(2,1)}, u32[]{:S(2)}, u32[]{:S(2)}) collective-permute-start(bf16[512,2048]{1,0:T(8,128)(2,1)} %get-tuple-element.32), channel_id=1, source_target_pairs={{0,2},{2,0},{4,6},{6,4},{8,10},{10,8},{12,14},{14,12},{16,18},{18,... | collective-permute-start | bytes 6291464 | tf_op jit(solution)/shard_map/ppermute | solution.py:204
  173.6 73.0 %collective-permute-start.12 = (bf16[4,512,256]{2,1,0:T(8,128)(2,1)}, bf16[4,512,256]{2,1,0:T(8,128)(2,1)}, u32[]{:S(2)}, u32[]{:S(2)}) collective-permute-start(bf16[4,512,256]{2,1,0:T(8,128)(2,1)} %code_pair.9), channel_id=1, source_target_pairs={{0,4},{2,6},{4,0},{6,2},{8,12},{10,14},{12,8},{14,10},{16,20},{18,... | collective-permute-start | bytes 3145736 | tf_op jit(solution)/shard_map/ppermute | solution.py:161
  184.7 66.0 %collective-permute-start.21 = (bf16[4,512,256]{2,1,0:T(8,128)(2,1)}, bf16[4,512,256]{2,1,0:T(8,128)(2,1)}, u32[]{:S(2)}, u32[]{:S(2)}) collective-permute-start(bf16[4,512,256]{2,1,0:T(8,128)(2,1)} %code_pair.11), channel_id=1, source_target_pairs={{0,4},{2,6},{4,0},{6,2},{8,12},{10,14},{12,8},{14,10},{16,20},{18,... | collective-permute-start | bytes 3145736 | tf_op jit(solution)/shard_map/ppermute | solution.py:161
  196.4 63.8 %collective-permute-start.30 = (bf16[4,512,256]{2,1,0:T(8,128)(2,1)}, bf16[4,512,256]{2,1,0:T(8,128)(2,1)}, u32[]{:S(2)}, u32[]{:S(2)}) collective-permute-start(bf16[4,512,256]{2,1,0:T(8,128)(2,1)} %code_pair.13), channel_id=1, source_target_pairs={{0,4},{2,6},{4,0},{6,2},{8,12},{10,14},{12,8},{14,10},{16,20},{18,... | collective-permute-start | bytes 3145736 | tf_op jit(solution)/shard_map/ppermute | solution.py:161
  207.6 73.8 %collective-permute-start.39 = (bf16[4,512,256]{2,1,0:T(8,128)(2,1)}, bf16[4,512,256]{2,1,0:T(8,128)(2,1)}, u32[]{:S(2)}, u32[]{:S(2)}) collective-permute-start(bf16[4,512,256]{2,1,0:T(8,128)(2,1)} %code_pair.15), channel_id=1, source_target_pairs={{0,4},{2,6},{4,0},{6,2},{8,12},{10,14},{12,8},{14,10},{16,20},{18,... | collective-permute-start | bytes 3145736 | tf_op jit(solution)/shard_map/ppermute | solution.py:161
  248.3 36.2 %collective-permute-start.14 = (bf16[512,256]{1,0:T(8,128)(2,1)S(1)}, bf16[512,256]{1,0:T(8,128)(2,1)S(1)}, u32[]{:S(2)}, u32[]{:S(2)}) collective-permute-start(bf16[512,256]{1,0:T(8,128)(2,1)S(1)} %get-tuple-element.55), channel_id=1, source_target_pairs={{0,16},{2,18},{4,20},{6,22},{8,24},{10,26},{12,28},{14,30},{16,0},... | collective-permute-start | bytes 786440 | tf_op jit(solution)/shard_map/ppermute | solution.py:161
  285.2 42.6 %collective-permute-start.32 = (bf16[512,256]{1,0:T(8,128)(2,1)S(1)}, bf16[512,256]{1,0:T(8,128)(2,1)S(1)}, u32[]{:S(2)}, u32[]{:S(2)}) collective-permute-start(bf16[512,256]{1,0:T(8,128)(2,1)S(1)} %get-tuple-element.49), channel_id=1, source_target_pairs={{0,16},{2,18},{4,20},{6,22},{8,24},{10,26},{12,28},{14,30},{16,0},... | collective-permute-start | bytes 786440 | tf_op jit(solution)/shard_map/ppermute | solution.py:161
  289.0 46.4 %collective-permute-start.33 = (bf16[512,256]{1,0:T(8,128)(2,1)S(1)}, bf16[512,256]{1,0:T(8,128)(2,1)S(1)}, u32[]{:S(2)}, u32[]{:S(2)}) collective-permute-start(bf16[512,256]{1,0:T(8,128)(2,1)S(1)} %get-tuple-element.48), channel_id=1, source_target_pairs={{0,24},{2,26},{4,28},{6,30},{8,0},{10,2},{12,4},{14,6},{16,8},{18,... | collective-permute-start | bytes 786440 | tf_op jit(solution)/shard_map/ppermute | solution.py:161
  296.1 40.6 %collective-permute-start.40 = (bf16[512,256]{1,0:T(8,128)(2,1)S(1)}, bf16[512,256]{1,0:T(8,128)(2,1)S(1)}, u32[]{:S(2)}, u32[]{:S(2)}) collective-permute-start(bf16[512,256]{1,0:T(8,128)(2,1)S(1)} %get-tuple-element.44), channel_id=1, source_target_pairs={{0,8},{2,10},{4,12},{6,14},{8,16},{10,18},{12,20},{14,22},{16,24},... | collective-permute-start | bytes 786440 | tf_op jit(solution)/shard_map/ppermute | solution.py:161
  303.3 46.1 %collective-permute-start.41 = (bf16[512,256]{1,0:T(8,128)(2,1)S(1)}, bf16[512,256]{1,0:T(8,128)(2,1)S(1)}, u32[]{:S(2)}, u32[]{:S(2)}) collective-permute-start(bf16[512,256]{1,0:T(8,128)(2,1)S(1)} %get-tuple-element.46), channel_id=1, source_target_pairs={{0,16},{2,18},{4,20},{6,22},{8,24},{10,26},{12,28},{14,30},{16,0},... | collective-permute-start | bytes 786440 | tf_op jit(solution)/shard_map/ppermute | solution.py:161
  313.5 44.5 %collective-permute-start.42 = (bf16[512,256]{1,0:T(8,128)(2,1)S(1)}, bf16[512,256]{1,0:T(8,128)(2,1)S(1)}, u32[]{:S(2)}, u32[]{:S(2)}) collective-permute-start(bf16[512,256]{1,0:T(8,128)(2,1)S(1)} %get-tuple-element.45), channel_id=1, source_target_pairs={{0,24},{2,26},{4,28},{6,30},{8,0},{10,2},{12,4},{14,6},{16,8},{18,... | collective-permute-start | bytes 786440 | tf_op jit(solution)/shard_map/ppermute | solution.py:161
  335.4 43.0 %collective-permute-start.64 = (bf16[512,256]{1,0:T(8,128)(2,1)S(1)}, bf16[512,256]{1,0:T(8,128)(2,1)S(1)}, u32[]{:S(2)}, u32[]{:S(2)}) collective-permute-start(bf16[512,256]{1,0:T(8,128)(2,1)S(1)} %get-tuple-element.20), channel_id=1, source_target_pairs={{0,16},{2,18},{4,20},{6,22},{8,24},{10,26},{12,28},{14,30},{16,0},... | collective-permute-start | bytes 786440 | tf_op jit(solution)/shard_map/ppermute | solution.py:161
  336.7 41.9 %collective-permute-start.65 = (bf16[512,256]{1,0:T(8,128)(2,1)S(1)}, bf16[512,256]{1,0:T(8,128)(2,1)S(1)}, u32[]{:S(2)}, u32[]{:S(2)}) collective-permute-start(bf16[512,256]{1,0:T(8,128)(2,1)S(1)} %get-tuple-element.20), channel_id=1, source_target_pairs={{0,8},{2,10},{4,12},{6,14},{8,16},{10,18},{12,20},{14,22},{16,24},... | collective-permute-start | bytes 786440 | tf_op jit(solution)/shard_map/ppermute | solution.py:161
  358.0 42.9 %collective-permute-start.58 = (bf16[512,256]{1,0:T(8,128)(2,1)S(1)}, bf16[512,256]{1,0:T(8,128)(2,1)S(1)}, u32[]{:S(2)}, u32[]{:S(2)}) collective-permute-start(bf16[512,256]{1,0:T(8,128)(2,1)S(1)} %get-tuple-element.22), channel_id=1, source_target_pairs={{0,16},{2,18},{4,20},{6,22},{8,24},{10,26},{12,28},{14,30},{16,0},... | collective-permute-start | bytes 786440 | tf_op jit(solution)/shard_map/ppermute | solution.py:161
  359.6 41.3 %collective-permute-start.59 = (bf16[512,256]{1,0:T(8,128)(2,1)S(1)}, bf16[512,256]{1,0:T(8,128)(2,1)S(1)}, u32[]{:S(2)}, u32[]{:S(2)}) collective-permute-start(bf16[512,256]{1,0:T(8,128)(2,1)S(1)} %get-tuple-element.22), channel_id=1, source_target_pairs={{0,8},{2,10},{4,12},{6,14},{8,16},{10,18},{12,20},{14,22},{16,24},... | collective-permute-start | bytes 786440 | tf_op jit(solution)/shard_map/ppermute | solution.py:161
  378.6 44.8 %collective-permute-start.52 = (bf16[512,256]{1,0:T(8,128)(2,1)S(1)}, bf16[512,256]{1,0:T(8,128)(2,1)S(1)}, u32[]{:S(2)}, u32[]{:S(2)}) collective-permute-start(bf16[512,256]{1,0:T(8,128)(2,1)S(1)} %get-tuple-element.24), channel_id=1, source_target_pairs={{0,16},{2,18},{4,20},{6,22},{8,24},{10,26},{12,28},{14,30},{16,0},... | collective-permute-start | bytes 786440 | tf_op jit(solution)/shard_map/ppermute | solution.py:161
  379.5 45.4 %collective-permute-start.53 = (bf16[512,256]{1,0:T(8,128)(2,1)S(1)}, bf16[512,256]{1,0:T(8,128)(2,1)S(1)}, u32[]{:S(2)}, u32[]{:S(2)}) collective-permute-start(bf16[512,256]{1,0:T(8,128)(2,1)S(1)} %get-tuple-element.24), channel_id=1, source_target_pairs={{0,8},{2,10},{4,12},{6,14},{8,16},{10,18},{12,20},{14,22},{16,24},... | collective-permute-start | bytes 786440 | tf_op jit(solution)/shard_map/ppermute | solution.py:161
  450.1 55.5 %collective-permute-start.55 = (bf16[4,512,256]{2,1,0:T(8,128)(2,1)S(1)}, bf16[4,512,256]{2,1,0:T(8,128)(2,1)}, u32[]{:S(2)}, u32[]{:S(2)}) collective-permute-start(bf16[4,512,256]{2,1,0:T(8,128)(2,1)S(1)} %pad_maximum_fusion.3.refs_0_), channel_id=1, source_target_pairs={{0,4},{2,6},{4,0},{6,2},{8,12},{10,14},{12,8},{14,10},{16,20},{18,... | collective-permute-start | bytes 3145736 | tf_op jit(solution)/shard_map/ppermute | solution.py:161
  460.5 66.6 %collective-permute-start.49 = (bf16[4,512,256]{2,1,0:T(8,128)(2,1)S(1)}, bf16[4,512,256]{2,1,0:T(8,128)(2,1)}, u32[]{:S(2)}, u32[]{:S(2)}) collective-permute-start(bf16[4,512,256]{2,1,0:T(8,128)(2,1)S(1)} %pad_maximum_fusion.2.refs_0_), channel_id=1, source_target_pairs={{0,4},{2,6},{4,0},{6,2},{8,12},{10,14},{12,8},{14,10},{16,20},{18,... | collective-permute-start | bytes 3145736 | tf_op jit(solution)/shard_map/ppermute | solution.py:161
  462.0 65.1 %collective-permute-start.68 = (bf16[4,512,256]{2,1,0:T(8,128)(2,1)S(1)}, bf16[4,512,256]{2,1,0:T(8,128)(2,1)S(1)}, u32[]{:S(2)}, u32[]{:S(2)}) collective-permute-start(bf16[4,512,256]{2,1,0:T(8,128)(2,1)S(1)} %collective-permute-done.67.refs_1_), channel_id=1, source_target_pairs={{0,2},{2,0},{4,6},{6,4},{8,10},{10,8},{12,14},{14,12},{16,18},{18,... | collective-permute-start | bytes 3145736 | tf_op jit(solution)/shard_map/ppermute | solution.py:204
  483.1 69.7 %collective-permute-start.54 = (bf16[4,512,256]{2,1,0:T(8,128)(2,1)S(1)}, bf16[4,512,256]{2,1,0:T(8,128)(2,1)}, u32[]{:S(2)}, u32[]{:S(2)}) collective-permute-start(bf16[4,512,256]{2,1,0:T(8,128)(2,1)S(1)} %pad_maximum_fusion.3.refs_0_), channel_id=1, source_target_pairs={{0,2},{2,0},{4,6},{6,4},{8,10},{10,8},{12,14},{14,12},{16,18},{18,... | collective-permute-start | bytes 3145736 | tf_op jit(solution)/shard_map/ppermute | solution.py:204
  483.1 78.2 %collective-permute-start.48 = (bf16[4,512,256]{2,1,0:T(8,128)(2,1)S(1)}, bf16[4,512,256]{2,1,0:T(8,128)(2,1)}, u32[]{:S(2)}, u32[]{:S(2)}) collective-permute-start(bf16[4,512,256]{2,1,0:T(8,128)(2,1)S(1)} %pad_maximum_fusion.2.refs_0_), channel_id=1, source_target_pairs={{0,2},{2,0},{4,6},{6,4},{8,10},{10,8},{12,14},{14,12},{16,18},{18,... | collective-permute-start | bytes 3145736 | tf_op jit(solution)/shard_map/ppermute | solution.py:204
  505.6 38.7 %collective-permute-start.62 = (bf16[4,512,256]{2,1,0:T(8,128)(2,1)}, bf16[4,512,256]{2,1,0:T(8,128)(2,1)}, u32[]{:S(2)}, u32[]{:S(2)}) collective-permute-start(bf16[4,512,256]{2,1,0:T(8,128)(2,1)} %collective-permute-done.61.refs_1_), channel_id=1, source_target_pairs={{0,2},{2,0},{4,6},{6,4},{8,10},{10,8},{12,14},{14,12},{16,18},{18,... | collective-permute-start | bytes 3145736 | tf_op jit(solution)/shard_map/ppermute | solution.py:204
  (81 other events, 2490.1 us)

commit v3 on v2

--- a/solution.py
+++ b/solution.py
@@ -107,16 +107,18 @@
 
 def merge_kernel(where_ref, *refs, groups):
     fresh, weights_ref, out_ref = refs[:groups], refs[groups], refs[-1]
-    slots, _, width = fresh[0].shape
-    for g in range(groups):
+    at = 1
+    for group in fresh:
+        slots, _, width = group.shape
         for s in range(slots):
-            lanes = pl.ds(pl.multiple_of(where_ref[1 + g * slots + s] * width, width), width)
-            both = f32(weights_ref[:, lanes]) * mix_share + f32(fresh[g][s]) * (1.0 - mix_share)
+            lanes = pl.ds(pl.multiple_of(where_ref[at] * width, width), width)
+            both = f32(weights_ref[:, lanes]) * mix_share + f32(group[s]) * (1.0 - mix_share)
             out_ref[:, lanes] = both.astype(out_ref.dtype)
+            at += 1
 
 
 def merge(where, fresh, weights, row, mine, so_far):
-    slots, rows, width = fresh[0].shape
+    _, rows, width = fresh[0].shape
     half = weights.shape[0] // 2
     tile = math.gcd(rows, row, MERGE_TILE)
 
@@ -125,7 +127,7 @@
 
     full = pl.BlockSpec((tile, weights.shape[1]), place)
     operands = [where, *fresh, weights]
-    in_specs = [pl.BlockSpec((slots, tile, width), lambda i, w: (0, i, 0))] * len(fresh) + [full]
+    in_specs = [pl.BlockSpec((group.shape[0], tile, width), lambda i, w: (0, i, 0)) for group in fresh] + [full]
     aliases = {}
     if so_far is not None:
         aliases = {len(operands): 0}
@@ -213,12 +215,13 @@
     parts = [slice(a, b) for a, b in zip(edges, edges[1:])]
 
     rounded = [halves(master, start).astype(jnp.bfloat16) for start in (mine, theirs)]
-    anchor = beside(rounded[0], swap(rounded[1]))
+    other = swap(rounded[1])
+    anchor = beside(rounded[0], other)
 
     heads = x_line.gather(anchor)
     rests = []
     for part in parts:
-        pieces = z_line.gather(anchor[part])
+        pieces = z_line.gather(beside(rounded[0][part], other[part]))
         rests.append(x_line.gather(jnp.stack(pieces[1:])))
 
     d = jnp.arange(z_length, dtype=jnp.int32)[None, :]
@@ -233,6 +236,7 @@
     offset = offset.astype(jnp.bfloat16)
     mate_offset = swap(halves(offset, theirs))
     mates = [swap(halves(weights, theirs + part.start, part.stop - part.start)) for part in parts]
+    master, momentum, _ = lax.optimization_barrier((master, momentum, rests[0][0]))
     pair_master = beside(halves(master, mine), swap(halves(master, theirs)))
     pair_momentum = beside(halves(momentum, mine), swap(halves(momentum, theirs)))
     key_values = project(hidden, weights)
@@ -254,10 +258,17 @@
         masters.append(new_master)
         momenta.append(new_momentum)
         pieces = z_line.gather(new_master.astype(jnp.bfloat16))
-        fresh.append(x_line.gather(jnp.stack(pieces)))
-        swapped.append([None] * x_length)
-        for g, group in enumerate(fresh[-1]):
-            swapped[-1][g] = swap(group)
+        ends = [[] for _ in range(x_length)]
+        if i == CHUNKS - 1:
+            for g, end in enumerate(x_line.gather(pieces[0][None])):
+                ends[g].append(end)
+        for g, end in enumerate(x_line.gather(jnp.stack(pieces[len(ends[0]) :]))):
+            ends[g].append(end)
+        swapped.append([])
+        for group in ends:
+            for end in group:
+                swapped[-1].append(swap(end))
+        fresh.append([end for group in ends for end in group])
 
     def home(pieces):
         pair = jnp.concatenate(pieces)

time: 566 us -> 579 us (1.023)
  local copies, waits for them, and re-layouts: 14.8 us -> 26 us
    ppermute x2, waiting for transfers between devices: 12.1 us -> 0.01 us  [shifted(): lax.ppermute(array, 'fsdp', [(i, (i + by) % share) for i in range(share)])]
    ppermute x49 -> x50, waiting for transfers between devices: 264 us -> 273 us  [send(): lax.ppermute(array, 'rep', [(i, target(i)) for i in range(self.total)])]
    ppermute x49 -> x50, starting transfers between devices: 131 us -> 127 us  [send(): lax.ppermute(array, 'rep', [(i, target(i)) for i in range(self.total)])]
  transfers between devices with their start and end apart: 69 -> 72, of which waited for: 24 -> 21; matrix products, arithmetic and copies ran while one was open for 7% -> 10% of each run, Pallas kernels for 18% -> 17%
where the time goes in v3:
time: 579 us; the launch traced here: 578 us
  waiting for transfers between devices  274 us (47%)
  starting transfers between devices  133 us (23%)
  Pallas kernels  104 us (18%)
  other arithmetic  31 us (5%)
  local copies, waits for them, and re-layouts  26 us (4%)
  matrix products  8.9 us (2%)
    ppermute x50, waiting for transfers between devices, send(): lax.ppermute(array, 'rep', [(i, target(i)) for i in range(self.total)])  273 us
    ppermute x50, starting transfers between devices, send(): lax.ppermute(array, 'rep', [(i, target(i)) for i in range(self.total)])  127 us
    pallas_call x8, Pallas kernels, code(): pl.pallas_call(functools.partial(code_kernel, strip=strip, first=group *...  70.3 us
    pallas_call x8, Pallas kernels, merge(): pl.pallas_call(functools.partial(merge_kernel, groups=len(fresh)), out_sh...  33.9 us
  transfers between devices with their start and end apart: 72, of which 21 were waited for; matrix products, arithmetic and copies ran while one was open for 10% of the time, Pallas kernels for 17%

profile of v3, /device:TPU:0, one launch (start us, length us, event | category | flops | bytes accessed | tf_op | source)
XLA Modules:
  0.0 578.4 jit_solution(14370963357669524684)
XLA Ops:
  19.1 7.5 %dynamic-slice_bitcast_fusion = (bf16[512,2048]{1,0:T(8,128)(2,1)}, bf16[512,2048]{1,0:T(8,128)(2,1)}, bf16[512,2048]{1,0:T(8,128)(2,1)}, bf16[512,2048]{1,0:T(8,128)(2,1)}) fusion(bf16[1,4096,2048]{2,1,0:T(8,128)(2,1)} %param.6, s32[]{:T(128)S(6)} %select_n.175, s32[]{:T(128)S(6)} %select_n.171, s32[]{:T(128)S(6)} %select_n.159, s32[]{:T(128)S(6)} %select_n.173), kind=kLoop, calls=%fused_computation.11 | loop fusion | bytes 16777232 | tf_op jit(solution)/shard_map/dynamic_slice | solution.py:209
  27.7 7.6 %collective-permute-done.4 = bf16[512,256]{1,0:T(8,128)(2,1)} collective-permute-done((bf16[512,256]{1,0:T(8,128)(2,1)}, bf16[512,256]{1,0:T(8,128)(2,1)}, u32[]{:S(2)}, u32[]{:S(2)}) %collective-permute-start.4) | collective-permute-done | bytes 262176 | tf_op jit(solution)/shard_map/ppermute | solution.py:163
  35.3 15.9 %collective-permute-start.26 = (bf16[512,256]{1,0:T(8,128)(2,1)S(1)}, bf16[512,256]{1,0:T(8,128)(2,1)S(1)}, u32[]{:S(2)}, u32[]{:S(2)}) collective-permute-start(bf16[512,256]{1,0:T(8,128)(2,1)S(1)} %maximum_select_fusion.7), channel_id=1, source_target_pairs={{0,16},{2,18},{4,20},{6,22},{8,24},{10,26},{12,28},{14,30},{16,0},... | collective-permute-start | bytes 786440 | tf_op jit(solution)/shard_map/ppermute | solution.py:163
  51.2 11.6 %collective-permute-done.17 = bf16[512,256]{1,0:T(8,128)(2,1)S(1)} collective-permute-done((bf16[512,256]{1,0:T(8,128)(2,1)}, bf16[512,256]{1,0:T(8,128)(2,1)S(1)}, u32[]{:S(2)}, u32[]{:S(2)}) %collective-permute-start.17) | collective-permute-done | bytes 262176 | tf_op jit(solution)/shard_map/ppermute | solution.py:163
  70.9 8.8 %collective-permute-done.26 = bf16[512,256]{1,0:T(8,128)(2,1)S(1)} collective-permute-done((bf16[512,256]{1,0:T(8,128)(2,1)S(1)}, bf16[512,256]{1,0:T(8,128)(2,1)S(1)}, u32[]{:S(2)}, u32[]{:S(2)}) %collective-permute-start.26) | collective-permute-done | bytes 262176 | tf_op jit(solution)/shard_map/ppermute | solution.py:163
  79.7 8.3 %collective-permute-start.35 = (bf16[512,256]{1,0:T(8,128)(2,1)S(1)}, bf16[512,256]{1,0:T(8,128)(2,1)S(1)}, u32[]{:S(2)}, u32[]{:S(2)}) collective-permute-start(bf16[512,256]{1,0:T(8,128)(2,1)S(1)} %maximum_select_fusion.8), channel_id=1, source_target_pairs={{0,16},{2,18},{4,20},{6,22},{8,24},{10,26},{12,28},{14,30},{16,0},... | collective-permute-start | bytes 786440 | tf_op jit(solution)/shard_map/ppermute | solution.py:163
  90.1 15.6 %collective-permute-done.35 = bf16[512,256]{1,0:T(8,128)(2,1)S(1)} collective-permute-done((bf16[512,256]{1,0:T(8,128)(2,1)S(1)}, bf16[512,256]{1,0:T(8,128)(2,1)S(1)}, u32[]{:S(2)}, u32[]{:S(2)}) %collective-permute-start.35) | collective-permute-done | bytes 262176 | tf_op jit(solution)/shard_map/ppermute | solution.py:163
  111.6 37.0 %collective-permute-done.11.rest_ref = bf16[3,512,256]{2,1,0:T(8,128)(2,1)S(1)} collective-permute-done((bf16[3,512,256]{2,1,0:T(8,128)(2,1)S(1)}, bf16[3,512,256]{2,1,0:T(8,128)(2,1)S(1)}, u32[]{:S(2)}, u32[]{:S(2)}) %collective-permute-start.11) | collective-permute-done | bytes 786464 | tf_op jit(solution)/shard_map/ppermute | solution.py:163
  150.3 15.1 %collective-permute-done.20.rest_ref = bf16[3,512,256]{2,1,0:T(8,128)(2,1)S(1)} collective-permute-done((bf16[3,512,256]{2,1,0:T(8,128)(2,1)S(1)}, bf16[3,512,256]{2,1,0:T(8,128)(2,1)S(1)}, u32[]{:S(2)}, u32[]{:S(2)}) %collective-permute-start.20) | collective-permute-done | bytes 786464 | tf_op jit(solution)/shard_map/ppermute | solution.py:163
  169.2 8.9 %code_pair.9 = bf16[4,512,256]{2,1,0:T(8,128)(2,1)} custom-call(s32[9]{0:T(128)} %pad_add_fusion.where_ref, bf16[2048,256]{1,0:T(8,128)(2,1)} %copy-done.4, bf16[3,512,256]{2,1,0:T(8,128)(2,1)} %copy-done.37, bf16[4096,2048]{1,0:T(8,128)(2,1)} %bitcast.108, bf16[4096,2048]{1,0:T(8,128)(2,1)} %bitcast.109, bf16[4096,2048]{1,0:T(8,128)(2,1)} %bitcast.110, ...), custom_call_target="tpu_custom_call" | custom-call | flops 41943040 | bytes 4194304 | tf_op jit(solution)/shard_map/code_pair/pallas_call | solution.py:90
  183.4 8.4 %fusion = f32[256,2048]{1,0:T(8,128)S(1)} fusion(bf16[128,4096]{1,0:T(8,128)(2,1)} %copy-done.41, bf16[128,4096]{1,0:T(8,128)(2,1)S(1)} %copy-done.28, bf16[1,4096,2048]{2,1,0:T(8,128)(2,1)} %param.6), kind=kOutput, calls=%fused_computation.1 | convolution fusion | flops 4299161600 | bytes 20971520 | tf_op jit(solution)/shard_map/dot_general | solution.py:186
  194.2 8.8 %code_pair.11 = bf16[4,512,256]{2,1,0:T(8,128)(2,1)} custom-call(s32[9]{0:T(128)} %pad_add_fusion.where_ref, bf16[2048,256]{1,0:T(8,128)(2,1)} %copy-done.4, bf16[3,512,256]{2,1,0:T(8,128)(2,1)} %copy-done.36, bf16[4096,2048]{1,0:T(8,128)(2,1)} %bitcast.112, bf16[4096,2048]{1,0:T(8,128)(2,1)} %bitcast.113, bf16[4096,2048]{1,0:T(8,128)(2,1)} %bitcast.114, ...), custom_call_target="tpu_custom_call" | custom-call | flops 41943040 | bytes 4194304 | tf_op jit(solution)/shard_map/code_pair/pallas_call | solution.py:90
  209.1 8.8 %code_pair.13 = bf16[4,512,256]{2,1,0:T(8,128)(2,1)} custom-call(s32[9]{0:T(128)} %pad_add_fusion.where_ref, bf16[2048,256]{1,0:T(8,128)(2,1)} %copy-done.4, bf16[3,512,256]{2,1,0:T(8,128)(2,1)} %collective-permute-done.29.rest_ref, bf16[4096,2048]{1,0:T(8,128)(2,1)} %bitcast.116, bf16[4096,2048]{1,0:T(8,128)(2,1)} %bitcast.117, ...), custom_call_target="tpu_custom_call" | custom-call | flops 41943040 | bytes 4194304 | tf_op jit(solution)/shard_map/code_pair/pallas_call | solution.py:90
  222.9 8.8 %code_pair.15 = bf16[4,512,256]{2,1,0:T(8,128)(2,1)} custom-call(s32[9]{0:T(128)} %pad_add_fusion.where_ref, bf16[2048,256]{1,0:T(8,128)(2,1)} %copy-done.4, bf16[3,512,256]{2,1,0:T(8,128)(2,1)} %collective-permute-done.38.rest_ref, bf16[4096,2048]{1,0:T(8,128)(2,1)} %bitcast.120, bf16[4096,2048]{1,0:T(8,128)(2,1)} %bitcast.121, ...), custom_call_target="tpu_custom_call" | custom-call | flops 41943040 | bytes 4194304 | tf_op jit(solution)/shard_map/code_pair/pallas_call | solution.py:90
  234.6 8.7 %code_pair.8 = bf16[4,512,256]{2,1,0:T(8,128)(2,1)} custom-call(s32[9]{0:T(128)} %pad_add_fusion.where_ref, bf16[2048,256]{1,0:T(8,128)(2,1)} %copy-done.3, bf16[3,512,256]{2,1,0:T(8,128)(2,1)} %copy-done.13, bf16[4096,2048]{1,0:T(8,128)(2,1)} %bitcast.126, bf16[4096,2048]{1,0:T(8,128)(2,1)} %bitcast.125, bf16[4096,2048]{1,0:T(8,128)(2,1)} %bitcast.124, ...), custom_call_target="tpu_custom_call" | custom-call | flops 41943040 | bytes 4194304 | tf_op jit(solution)/shard_map/code_pair/pallas_call | solution.py:90
  243.3 8.8 %code_pair.10 = bf16[4,512,256]{2,1,0:T(8,128)(2,1)} custom-call(s32[9]{0:T(128)} %pad_add_fusion.where_ref, bf16[2048,256]{1,0:T(8,128)(2,1)} %copy-done.3, bf16[3,512,256]{2,1,0:T(8,128)(2,1)} %copy-done.14, bf16[4096,2048]{1,0:T(8,128)(2,1)} %bitcast.128, bf16[4096,2048]{1,0:T(8,128)(2,1)} %bitcast.129, bf16[4096,2048]{1,0:T(8,128)(2,1)} %bitcast.130, ...), custom_call_target="tpu_custom_call" | custom-call | flops 41943040 | bytes 4194304 | tf_op jit(solution)/shard_map/code_pair/pallas_call | solution.py:90
  252.0 8.8 %code_pair.12 = bf16[4,512,256]{2,1,0:T(8,128)(2,1)} custom-call(s32[9]{0:T(128)} %pad_add_fusion.where_ref, bf16[2048,256]{1,0:T(8,128)(2,1)} %copy-done.3, bf16[3,512,256]{2,1,0:T(8,128)(2,1)} %copy-done.15, bf16[4096,2048]{1,0:T(8,128)(2,1)} %bitcast.132, bf16[4096,2048]{1,0:T(8,128)(2,1)} %bitcast.133, bf16[4096,2048]{1,0:T(8,128)(2,1)} %bitcast.134, ...), custom_call_target="tpu_custom_call" | custom-call | flops 41943040 | bytes 4194304 | tf_op jit(solution)/shard_map/code_pair/pallas_call | solution.py:90
  260.8 8.9 %code_pair.14 = bf16[4,512,256]{2,1,0:T(8,128)(2,1)} custom-call(s32[9]{0:T(128)} %pad_add_fusion.where_ref, bf16[2048,256]{1,0:T(8,128)(2,1)} %copy-done.3, bf16[3,512,256]{2,1,0:T(8,128)(2,1)} %pad_maximum_fusion.8.rest_ref, bf16[4096,2048]{1,0:T(8,128)(2,1)} %bitcast.136, bf16[4096,2048]{1,0:T(8,128)(2,1)} %bitcast.137, bf16[4096,2048]{1,0:T(8,128)(2,1)} %bitcast.138, ...), custom_call_target="tpu_custom_call" | custom-call | flops 41943040 | bytes 4194304 | tf_op jit(solution)/shard_map/code_pair/pallas_call | solution.py:90
  278.1 13.3 %collective-permute-done.39 = bf16[4,512,256]{2,1,0:T(8,128)(2,1)} collective-permute-done((bf16[4,512,256]{2,1,0:T(8,128)(2,1)}, bf16[4,512,256]{2,1,0:T(8,128)(2,1)}, u32[]{:S(2)}, u32[]{:S(2)}) %collective-permute-start.39) | collective-permute-done | bytes 1048608 | tf_op jit(solution)/shard_map/ppermute | solution.py:163
  297.0 11.4 %collective-permute-start.31 = (bf16[512,256]{1,0:T(8,128)(2,1)S(1)}, bf16[512,256]{1,0:T(8,128)(2,1)S(1)}, u32[]{:S(2)}, u32[]{:S(2)}) collective-permute-start(bf16[512,256]{1,0:T(8,128)(2,1)S(1)} %get-tuple-element.47), channel_id=1, source_target_pairs={{0,8},{2,10},{4,12},{6,14},{8,16},{10,18},{12,20},{14,22},{16,24},... | collective-permute-start | bytes 786440 | tf_op jit(solution)/shard_map/ppermute | solution.py:163
  313.0 11.6 %collective-permute-done.23 = bf16[512,256]{1,0:T(8,128)(2,1)S(1)} collective-permute-done((bf16[512,256]{1,0:T(8,128)(2,1)S(1)}, bf16[512,256]{1,0:T(8,128)(2,1)S(1)}, u32[]{:S(2)}, u32[]{:S(2)}) %collective-permute-start.23) | collective-permute-done | bytes 262176 | tf_op jit(solution)/shard_map/ppermute | solution.py:163
  327.9 5.9 %collective-permute-start.40 = (bf16[512,256]{1,0:T(8,128)(2,1)S(1)}, bf16[512,256]{1,0:T(8,128)(2,1)S(1)}, u32[]{:S(2)}, u32[]{:S(2)}) collective-permute-start(bf16[512,256]{1,0:T(8,128)(2,1)S(1)} %get-tuple-element.44), channel_id=1, source_target_pairs={{0,8},{2,10},{4,12},{6,14},{8,16},{10,18},{12,20},{14,22},{16,24},... | collective-permute-start | bytes 786440 | tf_op jit(solution)/shard_map/ppermute | solution.py:163
  335.5 11.8 %collective-permute-done.32 = bf16[512,256]{1,0:T(8,128)(2,1)S(1)} collective-permute-done((bf16[512,256]{1,0:T(8,128)(2,1)S(1)}, bf16[512,256]{1,0:T(8,128)(2,1)S(1)}, u32[]{:S(2)}, u32[]{:S(2)}) %collective-permute-start.32) | collective-permute-done | bytes 262176 | tf_op jit(solution)/shard_map/ppermute | solution.py:163
  348.6 10.0 %collective-permute-done.41 = bf16[512,256]{1,0:T(8,128)(2,1)S(1)} collective-permute-done((bf16[512,256]{1,0:T(8,128)(2,1)S(1)}, bf16[512,256]{1,0:T(8,128)(2,1)S(1)}, u32[]{:S(2)}, u32[]{:S(2)}) %collective-permute-start.41) | collective-permute-done | bytes 262176 | tf_op jit(solution)/shard_map/ppermute | solution.py:163
  372.8 13.2 %collective-permute-start.68 = (bf16[512,256]{1,0:T(8,128)(2,1)S(1)}, bf16[512,256]{1,0:T(8,128)(2,1)S(1)}, u32[]{:S(2)}, u32[]{:S(2)}) collective-permute-start(bf16[512,256]{1,0:T(8,128)(2,1)S(1)} %get-tuple-element.24), channel_id=1, source_target_pairs={{0,8},{2,10},{4,12},{6,14},{8,16},{10,18},{12,20},{14,22},{16,24},... | collective-permute-start | bytes 786440 | tf_op jit(solution)/shard_map/ppermute | solution.py:163
  386.0 16.3 %collective-permute-done.47 = bf16[512,256]{1,0:T(8,128)(2,1)S(1)} collective-permute-done((bf16[512,256]{1,0:T(8,128)(2,1)S(1)}, bf16[512,256]{1,0:T(8,128)(2,1)S(1)}, u32[]{:S(2)}, u32[]{:S(2)}) %collective-permute-start.47) | collective-permute-done | bytes 262176 | tf_op jit(solution)/shard_map/ppermute | solution.py:163
  403.8 15.9 %collective-permute-start.62 = (bf16[512,256]{1,0:T(8,128)(2,1)S(1)}, bf16[512,256]{1,0:T(8,128)(2,1)S(1)}, u32[]{:S(2)}, u32[]{:S(2)}) collective-permute-start(bf16[512,256]{1,0:T(8,128)(2,1)S(1)} %get-tuple-element.26), channel_id=1, source_target_pairs={{0,8},{2,10},{4,12},{6,14},{8,16},{10,18},{12,20},{14,22},{16,24},... | collective-permute-start | bytes 786440 | tf_op jit(solution)/shard_map/ppermute | solution.py:163
  424.9 16.7 %collective-permute-done.61 = bf16[512,256]{1,0:T(8,128)(2,1)S(1)} collective-permute-done((bf16[512,256]{1,0:T(8,128)(2,1)S(1)}, bf16[512,256]{1,0:T(8,128)(2,1)S(1)}, u32[]{:S(2)}, u32[]{:S(2)}) %collective-permute-start.61) | collective-permute-done | bytes 262176 | tf_op jit(solution)/shard_map/ppermute | solution.py:163
  443.8 13.3 %collective-permute-done.55 = bf16[512,256]{1,0:T(8,128)(2,1)S(1)} collective-permute-done((bf16[512,256]{1,0:T(8,128)(2,1)S(1)}, bf16[512,256]{1,0:T(8,128)(2,1)S(1)}, u32[]{:S(2)}, u32[]{:S(2)}) %collective-permute-start.55) | collective-permute-done | bytes 262176 | tf_op jit(solution)/shard_map/ppermute | solution.py:163
  459.3 27.6 %collective-permute-done.50.refs_2_ = bf16[1,512,256]{2,1,0:T(8,128)(2,1)} collective-permute-done((bf16[1,512,256]{2,1,0:T(8,128)(2,1)S(1)}, bf16[1,512,256]{2,1,0:T(8,128)(2,1)}, u32[]{:S(2)}, u32[]{:S(2)}) %collective-permute-start.50) | collective-permute-done | bytes 262176 | tf_op jit(solution)/shard_map/ppermute | solution.py:163
  489.7 23.2 %collective-permute-done.64.refs_1_ = bf16[4,512,256]{2,1,0:T(8,128)(2,1)S(1)} collective-permute-done((bf16[4,512,256]{2,1,0:T(8,128)(2,1)S(1)}, bf16[4,512,256]{2,1,0:T(8,128)(2,1)S(1)}, u32[]{:S(2)}, u32[]{:S(2)}) %collective-permute-start.64) | collective-permute-done | bytes 1048608 | tf_op jit(solution)/shard_map/ppermute | solution.py:163
  512.9 22.1 %collective-permute-done.58.refs_1_ = bf16[4,512,256]{2,1,0:T(8,128)(2,1)} collective-permute-done((bf16[4,512,256]{2,1,0:T(8,128)(2,1)S(1)}, bf16[4,512,256]{2,1,0:T(8,128)(2,1)}, u32[]{:S(2)}, u32[]{:S(2)}) %collective-permute-start.58) | collective-permute-done | bytes 1048608 | tf_op jit(solution)/shard_map/ppermute | solution.py:163
  (262 shorter events, 158.5 us)
Async XLA Ops:
  17.0 45.8 %collective-permute-start.17 = (bf16[512,256]{1,0:T(8,128)(2,1)}, bf16[512,256]{1,0:T(8,128)(2,1)S(1)}, u32[]{:S(2)}, u32[]{:S(2)}) collective-permute-start(bf16[512,256]{1,0:T(8,128)(2,1)} %maximum_select_fusion.6), channel_id=1, source_target_pairs={{0,16},{2,18},{4,20},{6,22},{8,24},{10,26},{12,28},{14,30},{16,0},... | collective-permute-start | bytes 786440 | tf_op jit(solution)/shard_map/ppermute | solution.py:163
  18.1 45.7 %collective-permute-start.18 = (bf16[512,256]{1,0:T(8,128)(2,1)}, bf16[512,256]{1,0:T(8,128)(2,1)S(1)}, u32[]{:S(2)}, u32[]{:S(2)}) collective-permute-start(bf16[512,256]{1,0:T(8,128)(2,1)} %maximum_select_fusion.6), channel_id=1, source_target_pairs={{0,8},{2,10},{4,12},{6,14},{8,16},{10,18},{12,20},{14,22},{16,24},... | collective-permute-start | bytes 786440 | tf_op jit(solution)/shard_map/ppermute | solution.py:163
  35.3 130.9 %collective-permute-start.8 = (bf16[512,2048]{1,0:T(8,128)(2,1)}, bf16[512,2048]{1,0:T(8,128)(2,1)S(1)}, u32[]{:S(2)}, u32[]{:S(2)}) collective-permute-start(bf16[512,2048]{1,0:T(8,128)(2,1)} %get-tuple-element.34), channel_id=1, source_target_pairs={{0,2},{2,0},{4,6},{6,4},{8,10},{10,8},{12,14},{14,12},{16,18},{18,... | collective-permute-start | bytes 6291464 | tf_op jit(solution)/shard_map/ppermute | solution.py:206
  35.3 44.4 %collective-permute-start.26 = (bf16[512,256]{1,0:T(8,128)(2,1)S(1)}, bf16[512,256]{1,0:T(8,128)(2,1)S(1)}, u32[]{:S(2)}, u32[]{:S(2)}) collective-permute-start(bf16[512,256]{1,0:T(8,128)(2,1)S(1)} %maximum_select_fusion.7), channel_id=1, source_target_pairs={{0,16},{2,18},{4,20},{6,22},{8,24},{10,26},{12,28},{14,30},{16,0},... | collective-permute-start | bytes 786440 | tf_op jit(solution)/shard_map/ppermute | solution.py:163
  69.4 39.4 %collective-permute-start = (bf16[128,4096]{1,0:T(8,128)(2,1)S(1)}, bf16[128,4096]{1,0:T(8,128)(2,1)S(1)}, u32[]{:S(2)}, u32[]{:S(2)}) collective-permute-start(bf16[128,4096]{1,0:T(8,128)(2,1)S(1)} %get-tuple-element.71), channel_id=1, source_target_pairs={{0,1},{1,0},{2,3},{3,2},{4,5},{5,4},{6,7},{7,6},{8,9},{9,8},{10,11... | collective-permute-start | bytes 3145736 | tf_op jit(solution)/shard_map/ppermute | solution.py:183
  79.7 103.1 %collective-permute-start.19 = (bf16[512,2048]{1,0:T(8,128)(2,1)}, bf16[512,2048]{1,0:T(8,128)(2,1)}, u32[]{:S(2)}, u32[]{:S(2)}) collective-permute-start(bf16[512,2048]{1,0:T(8,128)(2,1)} %get-tuple-element.33), channel_id=1, source_target_pairs={{0,2},{2,0},{4,6},{6,4},{8,10},{10,8},{12,14},{14,12},{16,18},{18,... | collective-permute-start | bytes 6291464 | tf_op jit(solution)/shard_map/ppermute | solution.py:206
  105.7 43.0 %collective-permute-start.10 = (bf16[2048,256]{1,0:T(8,128)(2,1)S(1)}, bf16[2048,256]{1,0:T(8,128)(2,1)S(1)}, u32[]{:S(2)}, u32[]{:S(2)}) collective-permute-start(bf16[2048,256]{1,0:T(8,128)(2,1)S(1)} %maximum_select_fusion.4.head_ref), channel_id=1, source_target_pairs={{0,4},{2,6},{4,0},{6,2},{8,12},{10,14},{12,8},{14,10},{16,20},{18,... | collective-permute-start | bytes 3145736 | tf_op jit(solution)/shard_map/ppermute | solution.py:163
  107.3 41.3 %collective-permute-start.11 = (bf16[3,512,256]{2,1,0:T(8,128)(2,1)S(1)}, bf16[3,512,256]{2,1,0:T(8,128)(2,1)S(1)}, u32[]{:S(2)}, u32[]{:S(2)}) collective-permute-start(bf16[3,512,256]{2,1,0:T(8,128)(2,1)S(1)} %pad_maximum_fusion.5.rest_ref), channel_id=1, source_target_pairs={{0,4},{2,6},{4,0},{6,2},{8,12},{10,14},{12,8},{14,10},{16,20},{18,... | collective-permute-start | bytes 2359304 | tf_op jit(solution)/shard_map/ppermute | solution.py:163
  108.8 56.6 %collective-permute-start.20 = (bf16[3,512,256]{2,1,0:T(8,128)(2,1)S(1)}, bf16[3,512,256]{2,1,0:T(8,128)(2,1)S(1)}, u32[]{:S(2)}, u32[]{:S(2)}) collective-permute-start(bf16[3,512,256]{2,1,0:T(8,128)(2,1)S(1)} %pad_maximum_fusion.6.rest_ref), channel_id=1, source_target_pairs={{0,4},{2,6},{4,0},{6,2},{8,12},{10,14},{12,8},{14,10},{16,20},{18,... | collective-permute-start | bytes 2359304 | tf_op jit(solution)/shard_map/ppermute | solution.py:163
  165.5 43.7 %collective-permute-start.28 = (bf16[512,2048]{1,0:T(8,128)(2,1)}, bf16[512,2048]{1,0:T(8,128)(2,1)}, u32[]{:S(2)}, u32[]{:S(2)}) collective-permute-start(bf16[512,2048]{1,0:T(8,128)(2,1)} %get-tuple-element.35), channel_id=1, source_target_pairs={{0,2},{2,0},{4,6},{6,4},{8,10},{10,8},{12,14},{14,12},{16,18},{18,... | collective-permute-start | bytes 6291464 | tf_op jit(solution)/shard_map/ppermute | solution.py:206
  166.2 56.8 %collective-permute-start.37 = (bf16[512,2048]{1,0:T(8,128)(2,1)}, bf16[512,2048]{1,0:T(8,128)(2,1)}, u32[]{:S(2)}, u32[]{:S(2)}) collective-permute-start(bf16[512,2048]{1,0:T(8,128)(2,1)} %get-tuple-element.32), channel_id=1, source_target_pairs={{0,2},{2,0},{4,6},{6,4},{8,10},{10,8},{12,14},{14,12},{16,18},{18,... | collective-permute-start | bytes 6291464 | tf_op jit(solution)/shard_map/ppermute | solution.py:206
  181.3 40.1 %collective-permute-start.38 = (bf16[3,512,256]{2,1,0:T(8,128)(2,1)}, bf16[3,512,256]{2,1,0:T(8,128)(2,1)}, u32[]{:S(2)}, u32[]{:S(2)}) collective-permute-start(bf16[3,512,256]{2,1,0:T(8,128)(2,1)} %pad_maximum_fusion.8.rest_ref), channel_id=1, source_target_pairs={{0,4},{2,6},{4,0},{6,2},{8,12},{10,14},{12,8},{14,10},{16,20},{18,... | collective-permute-start | bytes 2359304 | tf_op jit(solution)/shard_map/ppermute | solution.py:163
  182.9 86.9 %collective-permute-start.12 = (bf16[4,512,256]{2,1,0:T(8,128)(2,1)}, bf16[4,512,256]{2,1,0:T(8,128)(2,1)}, u32[]{:S(2)}, u32[]{:S(2)}) collective-permute-start(bf16[4,512,256]{2,1,0:T(8,128)(2,1)} %code_pair.9), channel_id=1, source_target_pairs={{0,4},{2,6},{4,0},{6,2},{8,12},{10,14},{12,8},{14,10},{16,20},{18,... | collective-permute-start | bytes 3145736 | tf_op jit(solution)/shard_map/ppermute | solution.py:163
  202.9 68.3 %collective-permute-start.21 = (bf16[4,512,256]{2,1,0:T(8,128)(2,1)}, bf16[4,512,256]{2,1,0:T(8,128)(2,1)}, u32[]{:S(2)}, u32[]{:S(2)}) collective-permute-start(bf16[4,512,256]{2,1,0:T(8,128)(2,1)} %code_pair.11), channel_id=1, source_target_pairs={{0,4},{2,6},{4,0},{6,2},{8,12},{10,14},{12,8},{14,10},{16,20},{18,... | collective-permute-start | bytes 3145736 | tf_op jit(solution)/shard_map/ppermute | solution.py:163
  217.9 54.9 %collective-permute-start.30 = (bf16[4,512,256]{2,1,0:T(8,128)(2,1)}, bf16[4,512,256]{2,1,0:T(8,128)(2,1)}, u32[]{:S(2)}, u32[]{:S(2)}) collective-permute-start(bf16[4,512,256]{2,1,0:T(8,128)(2,1)} %code_pair.13), channel_id=1, source_target_pairs={{0,4},{2,6},{4,0},{6,2},{8,12},{10,14},{12,8},{14,10},{16,20},{18,... | collective-permute-start | bytes 3145736 | tf_op jit(solution)/shard_map/ppermute | solution.py:163
  221.4 149.8 %collective-permute-start.1 = (f32[128,2048]{1,0:T(8,128)}, f32[128,2048]{1,0:T(8,128)}, u32[]{:S(2)}, u32[]{:S(2)}) collective-permute-start(f32[128,2048]{1,0:T(8,128)} %slice.217), channel_id=1, source_target_pairs={{0,1},{1,0},{2,3},{3,2},{4,5},{5,4},{6,7},{7,6},{8,9},{9,8},{10,11... | collective-permute-start | bytes 3145736 | tf_op jit(solution)/shard_map/ppermute | solution.py:183
  231.7 59.8 %collective-permute-start.39 = (bf16[4,512,256]{2,1,0:T(8,128)(2,1)}, bf16[4,512,256]{2,1,0:T(8,128)(2,1)}, u32[]{:S(2)}, u32[]{:S(2)}) collective-permute-start(bf16[4,512,256]{2,1,0:T(8,128)(2,1)} %code_pair.15), channel_id=1, source_target_pairs={{0,4},{2,6},{4,0},{6,2},{8,12},{10,14},{12,8},{14,10},{16,20},{18,... | collective-permute-start | bytes 3145736 | tf_op jit(solution)/shard_map/ppermute | solution.py:163
  297.0 38.1 %collective-permute-start.31 = (bf16[512,256]{1,0:T(8,128)(2,1)S(1)}, bf16[512,256]{1,0:T(8,128)(2,1)S(1)}, u32[]{:S(2)}, u32[]{:S(2)}) collective-permute-start(bf16[512,256]{1,0:T(8,128)(2,1)S(1)} %get-tuple-element.47), channel_id=1, source_target_pairs={{0,8},{2,10},{4,12},{6,14},{8,16},{10,18},{12,20},{14,22},{16,24},... | collective-permute-start | bytes 786440 | tf_op jit(solution)/shard_map/ppermute | solution.py:163
  309.6 37.6 %collective-permute-start.32 = (bf16[512,256]{1,0:T(8,128)(2,1)S(1)}, bf16[512,256]{1,0:T(8,128)(2,1)S(1)}, u32[]{:S(2)}, u32[]{:S(2)}) collective-permute-start(bf16[512,256]{1,0:T(8,128)(2,1)S(1)} %get-tuple-element.49), channel_id=1, source_target_pairs={{0,16},{2,18},{4,20},{6,22},{8,24},{10,26},{12,28},{14,30},{16,0},... | collective-permute-start | bytes 786440 | tf_op jit(solution)/shard_map/ppermute | solution.py:163
  364.4 37.9 %collective-permute-start.47 = (bf16[512,256]{1,0:T(8,128)(2,1)S(1)}, bf16[512,256]{1,0:T(8,128)(2,1)S(1)}, u32[]{:S(2)}, u32[]{:S(2)}) collective-permute-start(bf16[512,256]{1,0:T(8,128)(2,1)S(1)} %get-tuple-element.30), channel_id=1, source_target_pairs={{0,16},{2,18},{4,20},{6,22},{8,24},{10,26},{12,28},{14,30},{16,0},... | collective-permute-start | bytes 786440 | tf_op jit(solution)/shard_map/ppermute | solution.py:163
  367.0 36.8 %collective-permute-start.66 = (bf16[512,256]{1,0:T(8,128)(2,1)S(1)}, bf16[512,256]{1,0:T(8,128)(2,1)S(1)}, u32[]{:S(2)}, u32[]{:S(2)}) collective-permute-start(bf16[512,256]{1,0:T(8,128)(2,1)S(1)} %get-tuple-element.24), channel_id=1, source_target_pairs={{0,24},{2,26},{4,28},{6,30},{8,0},{10,2},{12,4},{14,6},{16,8},{18,... | collective-permute-start | bytes 786440 | tf_op jit(solution)/shard_map/ppermute | solution.py:163
  371.1 53.6 %collective-permute-start.67 = (bf16[512,256]{1,0:T(8,128)(2,1)S(1)}, bf16[512,256]{1,0:T(8,128)(2,1)S(1)}, u32[]{:S(2)}, u32[]{:S(2)}) collective-permute-start(bf16[512,256]{1,0:T(8,128)(2,1)S(1)} %get-tuple-element.24), channel_id=1, source_target_pairs={{0,16},{2,18},{4,20},{6,22},{8,24},{10,26},{12,28},{14,30},{16,0},... | collective-permute-start | bytes 786440 | tf_op jit(solution)/shard_map/ppermute | solution.py:163
  372.8 52.0 %collective-permute-start.68 = (bf16[512,256]{1,0:T(8,128)(2,1)S(1)}, bf16[512,256]{1,0:T(8,128)(2,1)S(1)}, u32[]{:S(2)}, u32[]{:S(2)}) collective-permute-start(bf16[512,256]{1,0:T(8,128)(2,1)S(1)} %get-tuple-element.24), channel_id=1, source_target_pairs={{0,8},{2,10},{4,12},{6,14},{8,16},{10,18},{12,20},{14,22},{16,24},... | collective-permute-start | bytes 786440 | tf_op jit(solution)/shard_map/ppermute | solution.py:163
  402.3 39.3 %collective-permute-start.61 = (bf16[512,256]{1,0:T(8,128)(2,1)S(1)}, bf16[512,256]{1,0:T(8,128)(2,1)S(1)}, u32[]{:S(2)}, u32[]{:S(2)}) collective-permute-start(bf16[512,256]{1,0:T(8,128)(2,1)S(1)} %get-tuple-element.26), channel_id=1, source_target_pairs={{0,16},{2,18},{4,20},{6,22},{8,24},{10,26},{12,28},{14,30},{16,0},... | collective-permute-start | bytes 786440 | tf_op jit(solution)/shard_map/ppermute | solution.py:163
  403.8 38.8 %collective-permute-start.62 = (bf16[512,256]{1,0:T(8,128)(2,1)S(1)}, bf16[512,256]{1,0:T(8,128)(2,1)S(1)}, u32[]{:S(2)}, u32[]{:S(2)}) collective-permute-start(bf16[512,256]{1,0:T(8,128)(2,1)S(1)} %get-tuple-element.26), channel_id=1, source_target_pairs={{0,8},{2,10},{4,12},{6,14},{8,16},{10,18},{12,20},{14,22},{16,24},... | collective-permute-start | bytes 786440 | tf_op jit(solution)/shard_map/ppermute | solution.py:163
  424.8 63.9 %collective-permute-start.44 = (f32[2048,128]{1,0:T(8,128)S(1)}, f32[2048,128]{1,0:T(8,128)S(1)}, u32[]{:S(2)}, u32[]{:S(2)}) collective-permute-start(f32[2048,128]{1,0:T(8,128)S(1)} %get-tuple-element.41), channel_id=1, source_target_pairs={{0,2},{2,0},{4,6},{6,4},{8,10},{10,8},{12,14},{14,12},{16,18},{18,... | collective-permute-start | bytes 3145736 | tf_op jit(solution)/shard_map/ppermute | solution.py:206
  441.6 45.2 %collective-permute-start.52 = (bf16[3,512,256]{2,1,0:T(8,128)(2,1)}, bf16[3,512,256]{2,1,0:T(8,128)(2,1)}, u32[]{:S(2)}, u32[]{:S(2)}) collective-permute-start(bf16[3,512,256]{2,1,0:T(8,128)(2,1)} %pad_maximum_fusion.9.refs_1_), channel_id=1, source_target_pairs={{0,4},{2,6},{4,0},{6,2},{8,12},{10,14},{12,8},{14,10},{16,20},{18,... | collective-permute-start | bytes 2359304 | tf_op jit(solution)/shard_map/ppermute | solution.py:163
  443.7 45.4 %collective-permute-start.43 = (f32[2048,128]{1,0:T(8,128)S(1)}, f32[2048,128]{1,0:T(8,128)S(1)}, u32[]{:S(2)}, u32[]{:S(2)}) collective-permute-start(f32[2048,128]{1,0:T(8,128)S(1)} %get-tuple-element.43), channel_id=1, source_target_pairs={{0,2},{2,0},{4,6},{6,4},{8,10},{10,8},{12,14},{14,12},{16,18},{18,... | collective-permute-start | bytes 3145736 | tf_op jit(solution)/shard_map/ppermute | solution.py:206
  488.8 46.2 %collective-permute-start.58 = (bf16[4,512,256]{2,1,0:T(8,128)(2,1)S(1)}, bf16[4,512,256]{2,1,0:T(8,128)(2,1)}, u32[]{:S(2)}, u32[]{:S(2)}) collective-permute-start(bf16[4,512,256]{2,1,0:T(8,128)(2,1)S(1)} %pad_maximum_fusion.2.refs_0_), channel_id=1, source_target_pairs={{0,4},{2,6},{4,0},{6,2},{8,12},{10,14},{12,8},{14,10},{16,20},{18,... | collective-permute-start | bytes 3145736 | tf_op jit(solution)/shard_map/ppermute | solution.py:163
  489.1 48.0 %collective-permute-start.63 = (bf16[4,512,256]{2,1,0:T(8,128)(2,1)S(1)}, bf16[4,512,256]{2,1,0:T(8,128)(2,1)S(1)}, u32[]{:S(2)}, u32[]{:S(2)}) collective-permute-start(bf16[4,512,256]{2,1,0:T(8,128)(2,1)S(1)} %pad_maximum_fusion.3.refs_0_), channel_id=1, source_target_pairs={{0,2},{2,0},{4,6},{6,4},{8,10},{10,8},{12,14},{14,12},{16,18},{18,... | collective-permute-start | bytes 3145736 | tf_op jit(solution)/shard_map/ppermute | solution.py:206
  489.2 48.6 %collective-permute-start.57 = (bf16[4,512,256]{2,1,0:T(8,128)(2,1)S(1)}, bf16[4,512,256]{2,1,0:T(8,128)(2,1)S(1)}, u32[]{:S(2)}, u32[]{:S(2)}) collective-permute-start(bf16[4,512,256]{2,1,0:T(8,128)(2,1)S(1)} %pad_maximum_fusion.2.refs_0_), channel_id=1, source_target_pairs={{0,2},{2,0},{4,6},{6,4},{8,10},{10,8},{12,14},{14,12},{16,18},{18,... | collective-permute-start | bytes 3145736 | tf_op jit(solution)/shard_map/ppermute | solution.py:206
  489.6 50.9 %collective-permute-start.71 = (bf16[4,512,256]{2,1,0:T(8,128)(2,1)S(1)}, bf16[4,512,256]{2,1,0:T(8,128)(2,1)S(1)}, u32[]{:S(2)}, u32[]{:S(2)}) collective-permute-start(bf16[4,512,256]{2,1,0:T(8,128)(2,1)S(1)} %collective-permute-done.70.refs_1_), channel_id=1, source_target_pairs={{0,2},{2,0},{4,6},{6,4},{8,10},{10,8},{12,14},{14,12},{16,18},{18,... | collective-permute-start | bytes 3145736 | tf_op jit(solution)/shard_map/ppermute | solution.py:206
  (82 other events, 2075.1 us)
